TPU v7x, 32 devices: a whole 2x2x4 slice. The times are simulated.
32 devices in a mesh: section: 2 (over core), tp: 4 (over y, x), pool: 4 (over z).
Axes of the slice: x: 2, y: 2, z: 4, core: 2. Of those that a mesh axis runs over, the one named last changes fastest.
Arguments:
- hidden: bfloat16 [2, 4, 128, 8192], P('section', 'pool', None, 'tp'), may hold values from -6 to 6
- queries: bfloat16 [2, 4, 16, 8, 64, 128], P('section', 'pool', None, None, 'tp'), may hold values from -450 to 450, as said below
- window_key_value: bfloat16 [2, 4, 16, 2, 8, 8, 128], P('section', 'pool', None, None, 'tp'), may hold values from -12 to 12
- cached_key_value: bfloat16 [2, 4, 128, 2, 8, 64, 128], P('section', 'pool', None, None, 'tp'), may hold values from -12 to 12
- cached_length: int32 [2, 4, 16], P('section', 'pool'), may hold values from 1 to 1024, 6144 in all within a row
- request_page_table: int32 [2, 4, 16, 16], P('section', 'pool'), may hold values from 0 to 127
- request_adapter: int32 [2, 4, 16], replicated, may hold values from 0 to 31, as said below
- layer_page_slot: int32 [64], replicated, may hold values from 0 to 63, as said below
- wo: bfloat16 [2, 8192, 8192], P('section', 'tp'), may hold values from -0.09375 to 0.09375
- adapter_down: bfloat16 [64, 64, 8192], P(('section', 'pool'), None, 'tp'), may hold values from -0.0625 to 0.0625
- adapter_up: bfloat16 [64, 64, 8192], P(('section', 'pool'), None, 'tp'), may hold values from -0.75 to 0.75
Outputs:
- next_hidden: bfloat16 [2, 4, 128, 8192], P('section', 'pool', None, 'tp')
Inputs may be any that keep to these rules, and one draw needn't show every extreme that they name: `queries`: queries of order one; some entries far larger in the hidden draw. `request_page_table`: several requests may name the same cache page; entries past a request's length are read but excluded. `cached_length`: each request of a device has 1 to 1024 cached positions. `layer_page_slot`: the adapters of layer s occupy slots s * 32 to (s + 1) * 32 - 1, each slot once; slot q lies on the index q // 8 of section and pool taken together, section first, so layer s's pages sit on section s. `request_adapter`: up to all 16 requests of a pool group may use adapters held on one pool index, and one pool index may serve every request of its section.
All inputs are finite; a program needn't handle non-finite values.
Results may differ from a plain program's by a relative error of at most 0.009.
Values may be sent and summed in bfloat16 or wider, within the bound.
No kernel may reach another device: no remote copies, remote signals or barrier semaphores. Data moves between devices by JAX's collectives and lax.ppermute only.
A program may use at most 192 MiB of HBM per device.

v0:
```python
import jax
import jax.numpy as jnp
from jax import lax
from jax.sharding import PartitionSpec as P


def from_behind(value, axis, steps):
    count = lax.axis_size(axis)
    pairs = [(source, (source + steps) % count) for source in range(count)]
    return lax.ppermute(value, axis, pairs)


def attend(queries, cache_pages, window_kv, lengths, page_rows):
    requests, window, head_count, head_size = queries.shape
    kv_heads = window_kv.shape[2]
    page_tok = cache_pages.shape[3]
    max_pages = page_rows.shape[1]
    cached = max_pages * page_tok
    picked = jnp.take(cache_pages, page_rows, axis=0)
    picked = jnp.transpose(picked, (0, 2, 3, 1, 4, 5)).reshape(
        requests, 2, kv_heads, cached, head_size
    )
    keys_all = jnp.concatenate([picked, window_kv], axis=3)
    grouped = queries.reshape(requests, window, kv_heads, head_count // kv_heads, head_size)
    scores = jnp.einsum(
        "rwkgd,rktd->rkgwt", grouped, keys_all[:, 0], preferred_element_type=jnp.float32
    ) * head_size ** (-0.5)
    position = jnp.arange(cached + window, dtype=jnp.int32)
    query_pos = jnp.arange(window, dtype=jnp.int32)
    in_cache = position[None, :] < lengths[:, None]
    in_window = (position[None, :] >= cached) & (position[None, :] - cached <= query_pos[:, None])
    allowed = in_cache[:, None, :] | in_window[None, :, :]
    scores = jnp.where(allowed[:, None, None, :, :], scores, -jnp.inf)
    largest = jnp.max(scores, axis=-1, keepdims=True)
    weights = jnp.exp(scores - largest)
    probs = (weights / jnp.sum(weights, axis=-1, keepdims=True)).astype(jnp.bfloat16)
    context = jnp.einsum(
        "rkgwt,rktd->rwkgd", probs, keys_all[:, 1], preferred_element_type=jnp.float32
    )
    return context.reshape(requests, window, head_count * head_size).astype(jnp.bfloat16)


def per_device(
    hidden,
    queries,
    window_key_value,
    cached_key_value,
    cached_length,
    request_page_table,
    request_adapter,
    layer_page_slot,
    wo,
    adapter_down,
    adapter_up,
):
    section_count = lax.axis_size("section")
    section_index = lax.axis_index("section")
    pool_index = lax.axis_index("pool")
    context = attend(
        queries[0, 0],
        cached_key_value[0, 0],
        window_key_value[0, 0],
        cached_length[0, 0],
        request_page_table[0, 0],
    )
    requests, window, width_of_head = context.shape
    flat_rows = context.reshape(requests * window, width_of_head)
    partial_out = jnp.dot(flat_rows, wo[0], preferred_element_type=jnp.float32)
    plain_output = lax.psum_scatter(partial_out, "tp", scatter_dimension=1, tiled=True)
    pages_per_member = adapter_down.shape[0]
    rank_width = adapter_down.shape[1]
    output_width = adapter_up.shape[2]
    adapters = layer_page_slot.shape[0] // section_count
    layer_start = section_index * adapters
    everyone = lax.all_gather(context, "pool", axis=0, tiled=True)
    total_requests = everyone.shape[0]
    all_slots = layer_page_slot[layer_start + request_adapter[section_index]].reshape(
        total_requests
    )
    local_slot = all_slots - layer_start - pool_index * pages_per_member
    owned_mask = (
        local_slot[:, None] == jnp.arange(pages_per_member, dtype=jnp.int32)[None, :]
    ).astype(jnp.float32)
    stacked_down = adapter_down.reshape(pages_per_member * rank_width, width_of_head)
    wide_rank = lax.dot_general(
        everyone, stacked_down, (((2,), (1,)), ((), ())), preferred_element_type=jnp.float32
    )
    wide_rank = wide_rank.reshape(total_requests, window, pages_per_member, rank_width)
    rank_hidden = jnp.sum(wide_rank * owned_mask[:, None, :, None], axis=2)
    rank_hidden = lax.psum(rank_hidden, "tp")
    broadcast_rows = (
        rank_hidden.astype(jnp.bfloat16)[:, :, None, :]
        * owned_mask.astype(jnp.bfloat16)[:, None, :, None]
    )
    broadcast_rows = broadcast_rows.reshape(total_requests * window, pages_per_member * rank_width)
    product = jnp.dot(
        broadcast_rows,
        adapter_up.reshape(pages_per_member * rank_width, output_width),
        preferred_element_type=jnp.float32,
    )
    returned = lax.all_to_all(
        product.astype(jnp.bfloat16), "pool", split_axis=0, concat_axis=0, tiled=True
    )
    adapter_delta = jnp.sum(
        returned.reshape(-1, requests * window, output_width).astype(jnp.float32), axis=0
    )
    blended_output = (hidden[0, 0].astype(jnp.float32) + plain_output + adapter_delta).astype(
        jnp.bfloat16
    )
    handed = from_behind(blended_output, "section", 1)
    return handed[None, None]


def solution(mesh):
    return jax.shard_map(
        per_device,
        mesh=mesh,
        in_specs=(
            P("section", "pool", None, "tp"),
            P("section", "pool", None, None, "tp", None),
            P("section", "pool", None, None, "tp", None, None),
            P("section", "pool", None, None, "tp", None, None),
            P("section", "pool", None),
            P("section", "pool", None, None),
            P(),
            P(),
            P("section", "tp", None),
            P(("section", "pool"), None, "tp"),
            P(("section", "pool"), None, "tp"),
        ),
        out_specs=P("section", "pool", None, "tp"),
        check_vma=False,
    )
```

profile of v0, /device:TPU:0, one launch (start us, length us, event | category | flops | bytes accessed | tf_op | source)
XLA Modules:
  0.0 203.5 jit_solution(5581836561486857038)
XLA Ops:
  7.4 0.0 copy-start
  7.4 0.0 all-gather.2.cloned.1.call-start
  7.4 0.8 compare_select_fusion
  8.2 0.7 compare_and_fusion
  8.9 0.1 reshape.214
  9.0 0.9 copy.39
  9.9 0.7 iota_compare_fusion
  10.7 13.1 %gather_fusion = bf16[256,2,2,64,128]{4,3,2,1,0:T(8,128)(2,1)} fusion(bf16[128,2,2,64,128]{4,3,2,1,0:T(8,128)(2,1)} %bitcast.84, s32[1024]{0:T(1024)S(1)} %pad_clamp_fusion.1), kind=kCustom, calls=%fused_computation | custom fusion | bytes 33555456 | tf_op jit(solution)/shard_map/jit(_take)/gather | solution.py:19
  23.8 0.0 copy-start.3
  23.8 14.2 %copy_select_fusion = bf16[16,16,2,2,64,128]{5,4,1,3,0,2:T(8,128)(2,1)} fusion(bf16[16,16,2,2,64,128]{5,4,3,2,1,0:T(8,128)(2,1)} %bitcast.83, pred[16,16]{1,0:T(8,128)(4,1)S(1)} %compare_and_fusion), kind=kLoop, calls=%fused_computation.7 | loop fusion | flops 8388608 | bytes 33554688 | tf_op jit(solution)/shard_map/jit(_take)/select_n | solution.py:19
  38.0 0.1 broadcast_or_fusion
  38.1 0.0 copy-done.3
  38.1 8.1 %fusion.38 = (f32[16,2,8,8]{2,3,1,0:T(8,128)S(1)}, f32[16,2,8,8,1032]{4,2,3,1,0:T(8,128)}) fusion(pred[16,8,1032]{2,1,0:T(8,128)(4,1)S(1)} %broadcast_or_fusion, bf16[16,2,2,8,128]{4,3,2,0,1:T(8,128)(2,1)S(1)} %bitcast.91, bf16[16,2,2,1024,128]{4,3,2,0,1:T(8,128)(2,1)} %bitcast.85, bf16[1,1,16,8,16,128]{5,4,3,2,1,0:T(8,128)(2,1)S(1)} %copy-done.3), kind=kOutput, calls=%fused_computation.56 | convolution fusion | flops 566428672 | bytes 26027008 | tf_op jit(solution)/shard_map/sub | solution.py:35
  46.3 7.1 %divide_convert_fusion = bf16[16,2,8,8,1032]{4,2,3,1,0:T(8,128)(2,1)} fusion(f32[16,2,8,8,1032]{4,2,3,1,0:T(8,128)} %get-tuple-element.8, f32[16,2,8,8]{2,3,1,0:T(8,128)S(1)} %get-tuple-element.7), kind=kLoop, calls=%fused_computation.9 | loop fusion | flops 4227072 | bytes 12689408 | tf_op jit(solution)/shard_map/convert_element_type | solution.py:36
  53.4 7.0 %fusion.23 = bf16[16,2,128,8,8]{2,4,3,1,0:T(8,128)(2,1)} fusion(bf16[16,2,8,8,1032]{4,2,3,1,0:T(8,128)(2,1)} %divide_convert_fusion, bf16[16,2,2,1024,128]{4,3,2,0,1:T(8,128)(2,1)} %bitcast.86, bf16[16,2,2,8,128]{4,3,2,0,1:T(8,128)(2,1)S(1)} %bitcast.92), kind=kOutput, calls=%fused_computation.29 | convolution fusion | flops 558235648 | bytes 21659648 | tf_op jit(solution)/shard_map/rkgwt,rktd->rwkgd/dot_general | solution.py:37
  60.4 0.0 all-gather.2.cloned.1.call-update
  60.5 0.2 reduce-scatter.2.cloned.1.call-start
  60.7 0.0 copy-start.2
  60.7 0.0 copy-start.1
  60.7 17.5 %fusion.1 = f32[128,8192]{1,0:T(8,128)} fusion(bf16[128,2048]{1,0:T(8,128)(2,1)} %bitcast.88, bf16[1,2048,8192]{2,1,0:T(8,128)(2,1)} %param.19), kind=kOutput, calls=%fused_computation.3 | convolution fusion | flops 4294967296 | bytes 38273024 | tf_op jit(solution)/shard_map/dot_general | solution.py:68
  78.2 0.0 reduce-scatter.2.cloned.1.call-update
  78.3 0.0 copy-done.2
  78.3 0.1 reshape.222
  78.4 0.0 copy-done.1
  78.4 0.8 gather_fusion.1
  79.2 0.1 fusion.32
  79.3 29.7 %all-gather.2.cloned.1.call-done = bf16[64,8,2048]{2,1,0:T(8,128)(2,1)} async-done(((bf16[16,8,2048]{2,1,0:T(8,128)(2,1)}), bf16[64,8,2048]{2,1,0:T(8,128)(2,1)}) %all-gather.2.cloned.1.call-update) | async-done | bytes 2097168 | tf_op jit(solution)/shard_map/all_gather | solution.py:75
  109.0 4.6 %multiply_reduce_fusion = f32[64,8,64]{2,1,0:T(8,128)S(1)} fusion(bf16[8,64,2048]{2,1,0:T(8,128)(2,1)} %param.20, bf16[64,8,2048]{2,1,0:T(8,128)(2,1)} %all-gather.2.cloned.1.call-done, f32[64,8]{1,0:T(8,128)S(1)} %get-tuple-element.5), kind=kOutput, calls=%fused_computation.28 | convolution fusion | flops 1074233344 | bytes 4327424 | tf_op jit(solution)/shard_map/dot_general | solution.py:85
  113.6 28.4 %all-reduce.1 = bf16[64,8,64]{2,1,0:T(8,128)(2,1)S(1)} all-reduce(f32[64,8,64]{2,1,0:T(8,128)S(1)} %multiply_reduce_fusion), channel_id=1, replica_groups=mesh['section'=2,'tp'=4,'pool'=4] {'tp'}, use_global_device_ids=true, to_apply=%region_4.5 | all-reduce | flops 32768 | bytes 196608 | tf_op jit(solution)/shard_map/psum | solution.py:90
  142.0 0.2 broadcast_multiply_fusion
  142.2 1.4 mul.56
  143.6 0.0 copy-done
  143.6 2.3 %convolution_convert_fusion = bf16[512,2048]{1,0:T(8,128)(2,1)S(1)} fusion(bf16[512,512]{1,0:T(8,128)(2,1)} %mul.56, bf16[512,2048]{1,0:T(8,128)(2,1)S(1)} %bitcast.82), kind=kOutput, calls=%fused_computation.24 | convolution fusion | flops 1074790400 | bytes 4718592 | tf_op jit(solution)/shard_map/dot_general | solution.py:96
  145.9 45.5 %all_to_all.9 = bf16[4,128,2048]{2,1,0:T(8,128)(2,1)S(1)} all-to-all(bf16[4,128,2048]{2,1,0:T(8,128)(2,1)S(1)} %bitcast.89), channel_id=1, replica_groups=mesh['section'=2,'tp'=4,'pool'=4] {'pool'}, dimensions={0} | all-to-all | bytes 4194304 | tf_op jit(solution)/shard_map/all_to_all | solution.py:101
  191.4 0.4 convert_reduce_fusion
  191.8 0.0 reduce-scatter.2.cloned.1.call-done
  191.8 1.5 fusion.29
  193.3 0.1 collective-permute-start
  193.4 1.9 collective-permute-done
  195.3 0.8 copy.43
  (7 shorter events, 0.1 us)
Async XLA Ops:
  7.4 136.2 %copy-start = (bf16[8,64,2048]{2,1,0:T(8,128)(2,1)S(1)}, bf16[8,64,2048]{2,1,0:T(8,128)(2,1)}, u32[]{:S(2)}) copy-start(bf16[8,64,2048]{2,1,0:T(8,128)(2,1)} %param.21) | copy-start | bytes 6291460
  7.4 101.6 %all-gather.2.cloned.1.call-start = ((), (), s32[]{:S(2)}) async-start(), calls=%async_computation.3 | async-start | bytes 2621440 | tf_op jit(solution)/shard_map/all_gather | solution.py:75
  23.8 14.3 %copy-start.3 = (bf16[1,1,16,8,16,128]{5,4,3,2,1,0:T(8,128)(2,1)S(1)}, bf16[1,1,16,8,16,128]{5,4,3,2,1,0:T(8,128)(2,1)}, u32[]{:S(2)}) copy-start(bf16[1,1,16,8,16,128]{5,4,3,2,1,0:T(8,128)(2,1)} %param.12) | copy-start | bytes 1572868
  60.5 131.3 %reduce-scatter.2.cloned.1.call-start = ((), (), s32[]{:S(2)}) async-start(), calls=%async_computation.2 | async-start | bytes 5242880 | tf_op jit(solution)/shard_map/reduce_scatter | solution.py:69
  60.7 17.6 %copy-start.2 = (s32[2,4,16]{2,1,0:T(4,128)S(1)}, s32[2,4,16]{2,1,0:T(4,128)}, u32[]{:S(2)}) copy-start(s32[2,4,16]{2,1,0:T(4,128)} %param.17) | copy-start | bytes 1540
  60.7 17.7 %copy-start.1 = (s32[64]{0:T(128)S(1)}, s32[64]{0:T(128)}, u32[]{:S(2)}) copy-start(s32[64]{0:T(128)} %param.18) | copy-start | bytes 772
  193.3 2.0 collective-permute-start
Sparse Core Ops, SparseCore 0:
  60.6 48.3 all-gather.1
Sparse Core Ops, SparseCore 1:
  78.3 60.4 reduce-scatter.1
where the time goes:
time: 204 us
  blocking collectives  73.9 us (36%)
  matrix products  39.6 us (19%)
  waiting for transfers between devices  31.7 us (16%)
  other arithmetic  25.9 us (13%)
  local copies, waits for them, and re-layouts  17.2 us (8%)
  between operations  15 us (7%)
    all_to_all x1, blocking collectives, per_device(): lax.all_to_all(product.astype(jnp.bfloat16), 'pool', split_axis=0, concat...  45.5 us
    all_gather x1, waiting for transfers between devices, per_device(): everyone = lax.all_gather(context, 'pool', axis=0, tiled=True)  29.7 us
    psum x1, blocking collectives, per_device(): rank_hidden = lax.psum(rank_hidden, 'tp')  28.4 us
    dot_general x1, matrix products, per_device(): partial_out = jnp.dot(flat_rows, wo[0], preferred_element_type=jnp.float32)  17.5 us
    select_n x2, other arithmetic, attend(): picked = jnp.take(cache_pages, page_rows, axis=0)  15 us
    gather x1, local copies, waits for them, and re-layouts, attend(): picked = jnp.take(cache_pages, page_rows, axis=0)  13.1 us
    sub x1, matrix products, attend(): weights = jnp.exp(scores - largest)  8.14 us
    convert_element_type x1, other arithmetic, attend(): (weights / jnp.sum(weights, axis=-1, keepdims=True)).astype(jnp.bfloat16)  7.14 us
  transfers between devices with their start and end apart: 3, of which 2 were waited for; matrix products, arithmetic and copies ran while one was open for 13% of the time, Pallas kernels for 0%

commit v1 on v0

v1 whole, which is shorter than its diff:
```python
import functools
import math

import jax
import jax.numpy as jnp
from jax import lax
from jax.experimental import pallas as pl
from jax.experimental.pallas import tpu as pltpu
from jax.sharding import PartitionSpec as P


CHUNKS = 2
KEY_BLOCK = 512
ITEMS = 2


def attend_kernel(first, lengths, pages, queries, window, cache, out, keys, sems, item_request, item_block, ordered, tops, sums, parts, wide, near_scores, far_scores, near_probs, far_probs):
    requests, rows_all, head_size = ordered.shape
    kv_heads = keys.shape[2]
    page_tok = cache.shape[3]
    window_len = window.shape[3]
    key_block = min(KEY_BLOCK, keys.shape[3])
    blocks = keys.shape[3] // key_block
    per_block = key_block // page_tok
    rows = rows_all // kv_heads
    heads_all = rows_all // window_len
    factor = head_size ** (-0.5) * math.log2(math.e)

    def page_copy(r, j):
        return pltpu.make_async_copy(
            cache.at[pages[first + r, j]],
            keys.at[r, :, :, pl.ds(pl.multiple_of(j * page_tok, page_tok), page_tok), :],
            sems.at[r, j],
        )

    def used_pages(r):
        return (lengths[first + r] + page_tok - 1) // page_tok

    def used_blocks(r):
        return (lengths[first + r] + key_block - 1) // key_block

    def start_request(r, items):
        count = used_pages(r)

        def one(j, c):
            page_copy(r, j).start()
            return c

        lax.fori_loop(0, count, one, 0)

        def clear(j, c):
            at = pl.ds(pl.multiple_of(j * page_tok, page_tok), page_tok)
            keys[r, 1, :, at, :] = jnp.zeros((kv_heads, page_tok, head_size), keys.dtype)
            return c

        lax.fori_loop(count, used_blocks(r) * per_block, clear, 0)

        def note(b, at):
            item_request[at] = r
            item_block[at] = b
            return at + 1

        return lax.fori_loop(0, used_blocks(r), note, items)

    items = lax.fori_loop(0, requests, start_request, 0)
    item_request[items] = 0
    item_block[items] = 0

    target = lax.broadcasted_iota(jnp.int32, (rows_all, rows_all), 0)
    source = lax.broadcasted_iota(jnp.int32, (rows_all, rows_all), 1)
    moved = (target % window_len) * heads_all + target // window_len
    permutation = jnp.where(source == moved, 1.0, 0.0).astype(jnp.bfloat16)

    def prepare(r, carry):
        ordered[r] = jnp.dot(
            permutation, queries[r], preferred_element_type=jnp.float32
        ).astype(jnp.bfloat16)
        return carry

    lax.fori_loop(0, requests, prepare, 0, unroll=4)

    last = (((1,), (1,)), ((), ()))
    win_cols = requests * window_len
    win_col = lax.broadcasted_iota(jnp.int32, (rows, win_cols), 1)
    win_row = lax.broadcasted_iota(jnp.int32, (rows, win_cols), 0)
    win_of = jnp.where((win_col % window_len) <= (win_row % window_len), win_col // window_len, -1)
    col = lax.broadcasted_iota(jnp.int32, (rows, key_block), 1)
    win_keys = []
    win_values = []
    for k in range(kv_heads):
        for store, kind in ((win_keys, 0), (win_values, 1)):
            taken = window[:, kind, k].astype(jnp.float32).reshape(win_cols, head_size)
            store.append(taken.astype(jnp.bfloat16))

    def item_step(i, carry):
        work = []
        for u in range(ITEMS):
            at = jnp.minimum(i * ITEMS + u, items)
            real = at < items
            r, b = item_request[at], item_block[at]
            stop = jnp.where(real, jnp.minimum(used_pages(r), (b + 1) * per_block), 0)

            def arrive(j, c, r=r):
                page_copy(r, j).wait()
                return c

            lax.fori_loop(b * per_block, stop, arrive, 0)
            work.append((r, b, jnp.where(real, r * blocks + b, requests * blocks)))
        chains = [(u, k) for u in range(ITEMS) for k in range(kv_heads)]
        peaks = {}
        for u, k in chains:
            r, b, slot = work[u]
            span = pl.ds(pl.multiple_of(b * key_block, key_block), key_block)
            asked = ordered[r, k * rows : (k + 1) * rows, :]
            near = lax.dot_general(asked, win_keys[k], last, preferred_element_type=jnp.float32)
            far = lax.dot_general(
                asked, keys[r, 0, k, span, :], last, preferred_element_type=jnp.float32
            )
            near = jnp.where(win_of == jnp.where(b == 0, r, requests), near, -jnp.inf)
            far = jnp.where(col < lengths[first + r] - b * key_block, far, -jnp.inf)
            near_scores[u, k] = near
            far_scores[u, k] = far
            peaks[u, k] = jnp.maximum(
                jnp.max(near, axis=-1, keepdims=True), jnp.max(far, axis=-1, keepdims=True)
            )
        for u, k in chains:
            slot = work[u][2]
            top = peaks[u, k]
            near = jnp.exp2((near_scores[u, k] - top) * factor)
            far = jnp.exp2((far_scores[u, k] - top) * factor)
            near_probs[u, k] = near.astype(jnp.bfloat16)
            far_probs[u, k] = far.astype(jnp.bfloat16)
            total = jnp.sum(near, axis=-1, keepdims=True) + jnp.sum(far, axis=-1, keepdims=True)
            tops[slot, k] = jnp.broadcast_to(top, (rows, head_size))
            sums[slot, k] = jnp.broadcast_to(total, (rows, head_size))
        for u, k in chains:
            r, b, slot = work[u]
            span = pl.ds(pl.multiple_of(b * key_block, key_block), key_block)
            parts[slot, k] = jnp.dot(
                far_probs[u, k], keys[r, 1, k, span, :], preferred_element_type=jnp.float32
            ) + jnp.dot(near_probs[u, k], win_values[k], preferred_element_type=jnp.float32)
        return carry

    lax.fori_loop(0, (items + ITEMS - 1) // ITEMS, item_step, 0)

    def combine(r, carry):
        count = used_blocks(r)
        at = pl.ds(pl.multiple_of(r * window_len, window_len), window_len)
        for k in range(kv_heads):
            top = tops[r * blocks, k]
            for b in range(1, blocks):
                top = jnp.where(b < count, jnp.maximum(top, tops[r * blocks + b, k]), top)
            total, value = 0.0, 0.0
            for b in range(blocks):
                share = jnp.exp2((tops[r * blocks + b, k] - top) * factor)
                added = sums[r * blocks + b, k] * share
                moved = parts[r * blocks + b, k] * share
                total = total + (added if b == 0 else jnp.where(b < count, added, 0.0))
                value = value + (moved if b == 0 else jnp.where(b < count, moved, 0.0))
            value = value / total
            for g in range(rows // window_len):
                start = (k * (rows // window_len) + g) * head_size
                wide[at, start : start + head_size] = value[g * window_len : (g + 1) * window_len]
        return carry

    lax.fori_loop(0, requests, combine, 0, unroll=2)
    out[...] = wide[...].astype(out.dtype)


def attend(first, requests, queries, window, cache, lengths, pages):
    _, window_len, heads, head_size = queries.shape
    kv_heads, page_tok = cache.shape[2], cache.shape[3]
    max_keys = pages.shape[1] * page_tok
    rows_all = window_len * heads
    rows = rows_all // kv_heads
    slots = requests * (max_keys // min(KEY_BLOCK, max_keys)) + 1
    flat = queries.reshape(queries.shape[0], rows_all, head_size)
    smem = pl.BlockSpec(memory_space=pltpu.SMEM)
    take = first // requests
    return pl.pallas_call(
        functools.partial(attend_kernel, first),
        grid=(1,),
        in_specs=[
            smem,
            smem,
            pl.BlockSpec((requests, rows_all, head_size), lambda i: (take, 0, 0)),
            pl.BlockSpec((requests,) + window.shape[1:], lambda i: (take, 0, 0, 0, 0)),
            pl.BlockSpec(memory_space=pl.ANY),
        ],
        out_specs=pl.BlockSpec((requests * window_len, heads * head_size), lambda i: (0, 0)),
        out_shape=jax.ShapeDtypeStruct((requests * window_len, heads * head_size), jnp.bfloat16),
        scratch_shapes=[
            pltpu.VMEM((requests, 2, kv_heads, max_keys, head_size), jnp.bfloat16),
            pltpu.SemaphoreType.DMA((requests, pages.shape[1])),
            pltpu.SMEM((slots + 1,), jnp.int32),
            pltpu.SMEM((slots + 1,), jnp.int32),
            pltpu.VMEM((requests, rows_all, head_size), jnp.bfloat16),
            pltpu.VMEM((slots, kv_heads, rows, head_size), jnp.float32),
            pltpu.VMEM((slots, kv_heads, rows, head_size), jnp.float32),
            pltpu.VMEM((slots, kv_heads, rows, head_size), jnp.float32),
            pltpu.VMEM((requests * window_len, heads * head_size), jnp.float32),
            pltpu.VMEM((ITEMS, kv_heads, rows, requests * window_len), jnp.float32),
            pltpu.VMEM((ITEMS, kv_heads, rows, min(KEY_BLOCK, max_keys)), jnp.float32),
            pltpu.VMEM((ITEMS, kv_heads, rows, requests * window_len), jnp.bfloat16),
            pltpu.VMEM((ITEMS, kv_heads, rows, min(KEY_BLOCK, max_keys)), jnp.bfloat16),
        ],
        cost_estimate=pl.CostEstimate(flops=500000000, bytes_accessed=12000000, transcendentals=0),
        name="attend",
    )(lengths, pages, flat, window, cache)


def project_kernel(piece, *refs):
    count = len(refs) - 5
    rows, weights, out = refs[:count], refs[count], refs[count + 1]
    held, stored, sems = refs[count + 2 :]
    blocks, _, block = stored.shape
    each = held.shape[0] // count
    start = piece[0] * (blocks * block)

    def row_copy(i):
        return pltpu.make_async_copy(
            rows[i], held.at[pl.ds(i * each, each)], sems.at[blocks + i]
        )

    def weight_copy(b):
        at = pl.ds(pl.multiple_of(start + b * block, block), block)
        return pltpu.make_async_copy(weights.at[:, at], stored.at[b], sems.at[b])

    for i in range(count):
        row_copy(i).start()
    for b in range(blocks):
        weight_copy(b).start()
    for i in range(count):
        row_copy(i).wait()

    def step(b, carry):
        weight_copy(b).wait()
        at = pl.ds(pl.multiple_of(b * block, block), block)
        out[:, at] = jnp.dot(
            held[...], stored[b], preferred_element_type=jnp.float32
        ).astype(out.dtype)
        return carry

    lax.fori_loop(0, blocks, step, 0)


def project(chunks, weights, piece, pieces):
    depth, width = weights.shape
    own = width // pieces
    block = min(256, own)
    blocks = own // block
    total = sum(c.shape[0] for c in chunks)
    anywhere = pl.BlockSpec(memory_space=pl.ANY)
    return pl.pallas_call(
        project_kernel,
        in_specs=[pl.BlockSpec(memory_space=pltpu.SMEM)] + [anywhere] * (len(chunks) + 1),
        out_specs=pl.BlockSpec(memory_space=pltpu.VMEM),
        out_shape=jax.ShapeDtypeStruct((total, own), jnp.bfloat16),
        scratch_shapes=[
            pltpu.VMEM((total, depth), jnp.bfloat16),
            pltpu.VMEM((blocks, depth, block), jnp.bfloat16),
            pltpu.SemaphoreType.DMA((blocks + len(chunks),)),
        ],
        cost_estimate=pl.CostEstimate(
            flops=2 * total * depth * own,
            bytes_accessed=2 * (depth * own + total * (depth + own)),
            transcendentals=0,
        ),
        name="project",
    )(jnp.reshape(piece, (1,)).astype(jnp.int32), *chunks, weights)


def pick(table, index):
    value = jnp.int32(table[0])
    for i in range(1, len(table)):
        value = jnp.where(index == i, jnp.int32(table[i]), value)
    return value


def local_slots(where, adapters_of, slot_of, order, steps, first, count, pages_here):
    section, pool = where[0], where[1]
    adapters = slot_of.shape[0] // adapters_of.shape[0]
    place_of = [order.index(p) for p in range(len(order))]
    place = pick(place_of, pool)
    slots = []
    for step in steps:
        group = pick(order, lax.rem(place - step + len(order), len(order)))
        for r in range(count):
            slot = slot_of[section * adapters + adapters_of[section, group, first + r]]
            slots.append(slot - section * adapters - pool * pages_here)
    return slots


def rank_kernel(order, steps, first, count, where, adapters_of, slot_of, down, *refs):
    held, out = refs[:-1], refs[-1]
    pages_here, rank_width, features = down.shape
    wide_cols = pages_here * rank_width
    lanes = out.shape[1]
    slots = local_slots(where, adapters_of, slot_of, order, steps, first, count, pages_here)
    rows = jnp.concatenate([h[...] for h in held], axis=0)
    wide = lax.dot_general(
        rows, down[...].reshape(wide_cols, features), (((1,), (1,)), ((), ())),
        preferred_element_type=jnp.float32,
    )
    window_len = rows.shape[0] // len(slots)
    page = lax.broadcasted_iota(jnp.int32, (window_len, wide_cols), 1) // rank_width
    folded = []
    for i, slot in enumerate(slots):
        kept = jnp.where(page == slot, wide[i * window_len : (i + 1) * window_len], 0.0)
        total = kept[:, :lanes]
        for start in range(lanes, wide_cols, lanes):
            total = total + kept[:, start : start + lanes]
        folded.append(total)
    out[...] = jnp.concatenate(folded, axis=0).astype(out.dtype)


def up_kernel(order, first, count, parts, where, adapters_of, slot_of, up, *refs):
    ranks, outs = refs[:parts], refs[parts:]
    pages_here, rank_width, features = up.shape
    wide_cols = pages_here * rank_width
    lanes = ranks[0].shape[1]
    steps = range(len(order))
    slots = local_slots(where, adapters_of, slot_of, order, steps, first, count, pages_here)
    total = ranks[0][...].astype(jnp.float32)
    for other in ranks[1:]:
        total = total + other[...].astype(jnp.float32)
    window_len = total.shape[0] // len(slots)
    page = lax.broadcasted_iota(jnp.int32, (window_len, wide_cols), 1) // rank_width
    spread = []
    for i, slot in enumerate(slots):
        block = total[i * window_len : (i + 1) * window_len]
        tiled = jnp.concatenate([block] * (wide_cols // lanes), axis=1)
        spread.append(jnp.where(page == slot, tiled, 0.0))
    spread = jnp.concatenate(spread, axis=0).astype(jnp.bfloat16)
    weights = up[...].reshape(wide_cols, features)
    each = outs[0].shape[0]
    block = min(512, features)
    for start in range(0, features, block):
        made = jnp.dot(
            spread, weights[:, start : start + block], preferred_element_type=jnp.float32
        ).astype(jnp.bfloat16)
        for i, out in enumerate(outs):
            out[:, start : start + block] = made[i * each : (i + 1) * each]


def small_call(kernel, where, adapters_of, slot_of, weights, arrays, outs, flops):
    smem = pl.BlockSpec(memory_space=pltpu.SMEM)

    def whole(x):
        return pl.BlockSpec(x.shape, lambda i: (0,) * len(x.shape))

    moved = weights.size + sum(x.size for x in arrays)
    return pl.pallas_call(
        kernel,
        grid=(1,),
        in_specs=[smem] * 3 + [whole(weights)] + [whole(x) for x in arrays],
        out_specs=[whole(x) for x in outs],
        out_shape=outs,
        cost_estimate=pl.CostEstimate(flops=flops, bytes_accessed=2 * moved, transcendentals=0),
    )(where, adapters_of, slot_of, weights, *arrays)


def after(value, *earlier):
    return lax.optimization_barrier((value,) + earlier)[0]


def per_device(
    hidden,
    queries,
    window_key_value,
    cached_key_value,
    cached_length,
    request_page_table,
    request_adapter,
    layer_page_slot,
    wo,
    adapter_down,
    adapter_up,
):
    sections = lax.axis_size("section")
    pools = lax.axis_size("pool")
    splits = lax.axis_size("tp")
    section = lax.axis_index("section")
    pool = lax.axis_index("pool")
    split = lax.axis_index("tp")
    groups = queries.shape[2]
    window_len = queries.shape[3]
    part = groups // CHUNKS
    part_rows = part * window_len
    pages_here, rank_width, features = adapter_down.shape
    own_width = adapter_up.shape[2]
    wide_cols = pages_here * rank_width

    order = list(range(0, pools, 2)) + list(range(1, pools, 2))[::-1]
    ring = [(order[i], order[(i + 1) % pools]) for i in range(pools)]
    ring_next = [
        (s * pools + a, ((s + 1) % sections) * pools + b) for s in range(sections) for a, b in ring
    ]
    forward = [(s, (s + 1) % sections) for s in range(sections)]
    where = jnp.stack([section, pool]).astype(jnp.int32)

    def attend_part(c, asked):
        return attend(
            c * part,
            part,
            asked,
            window_key_value[0, 0],
            cached_key_value[0, 0],
            cached_length[0, 0],
            request_page_table[0, 0],
        )

    def gather(value):
        return lax.ppermute(value, "pool", ring)

    offsets = list(range(splits - 1, 0, -1)) + [0]

    def project_piece(i, *earlier):
        d = offsets[i]
        first = after(contexts[0], *earlier)
        piece = project([first] + contexts[1:], wo[0], split ^ d, splits)
        pairs = [
            (s * splits + t, ((s + 1) % sections) * splits + (t ^ d))
            for s in range(sections)
            for t in range(splits)
        ]
        arrived.append(lax.ppermute(piece, ("section", "tp"), pairs))
        return piece

    lanes = min(128, wide_cols)

    def rank_of(c, earlier):
        arrays = [after(held[c][0], earlier)] + held[c][1:]
        return small_call(
            functools.partial(rank_kernel, order, list(range(pools)), c * part, part),
            where,
            request_adapter,
            layer_page_slot,
            adapter_down,
            arrays,
            [jax.ShapeDtypeStruct((pools * part_rows, lanes), jnp.bfloat16)],
            2 * pools * part_rows * wide_cols * features,
        )[0]

    def up_of(c, mine, earlier):
        ranks = [after(mine, earlier)]
        for d in range(splits - 1, 0, -1):
            pairs = [(t, t ^ d) for t in range(splits)]
            ranks.append(lax.ppermute(mine, "tp", pairs))
        outs = small_call(
            functools.partial(up_kernel, order, c * part, part, len(ranks)),
            where,
            request_adapter,
            layer_page_slot,
            adapter_up,
            ranks,
            [jax.ShapeDtypeStruct((part_rows, own_width), jnp.bfloat16)] * pools,
            2 * pools * part_rows * wide_cols * own_width,
        )
        return outs

    def scatter(step, value):
        if step == pools - 1:
            return lax.ppermute(value, ("section", "pool"), ring_next)
        return lax.ppermute(value, "pool", ring)

    hidden_in = lax.ppermute(hidden[0, 0], "section", forward)
    arrived = []
    contexts = [attend_part(0, queries[0, 0])]
    contexts.append(attend_part(1, after(queries[0, 0], contexts[0])))
    held = [[c] for c in contexts]
    held[0].append(gather(contexts[0]))
    held[0].append(gather(held[0][1]))
    held[1].append(gather(contexts[1]))
    piece = project_piece(0, held[0][1])
    held[0].append(gather(after(held[0][2], piece)))
    piece = project_piece(1, piece, held[0][2])
    held[1].append(gather(after(held[1][1], piece)))
    piece = project_piece(2, piece, held[1][1])
    for _ in range(4, pools):
        held[0].append(gather(held[0][-1]))
    rank0 = rank_of(0, piece)
    held[1].append(gather(after(held[1][2], rank0)))
    for _ in range(4, pools):
        held[1].append(gather(held[1][-1]))
    outs0 = up_of(0, rank0, held[1][2])
    own0 = lax.ppermute(outs0[0], "section", forward)
    moving0 = scatter(1, outs0[1])
    rank1 = rank_of(1, outs0[0])
    moving0 = scatter(2, after(moving0, rank1) + outs0[2])
    outs1 = up_of(1, rank1, rank1)
    own1 = lax.ppermute(outs1[0], "section", forward)
    moving1 = scatter(1, outs1[1])
    piece = project_piece(3, piece, outs1[0])
    moving0 = scatter(3, after(moving0, piece) + outs0[3])
    moving1 = scatter(2, after(moving1, piece) + outs1[2])
    moving1 = scatter(3, moving1 + outs1[3])
    for step in range(4, pools):
        moving0 = scatter(step, moving0 + outs0[step])
        moving1 = scatter(step, moving1 + outs1[step])

    base = hidden_in.astype(jnp.float32)
    for piece in arrived:
        base = base + piece.astype(jnp.float32)
    delta = jnp.concatenate(
        [
            own0.astype(jnp.float32) + moving0.astype(jnp.float32),
            own1.astype(jnp.float32) + moving1.astype(jnp.float32),
        ]
    )
    return (base + delta).astype(jnp.bfloat16)[None, None]


def solution(mesh):
    return jax.shard_map(
        per_device,
        mesh=mesh,
        in_specs=(
            P("section", "pool", None, "tp"),
            P("section", "pool", None, None, "tp", None),
            P("section", "pool", None, None, "tp", None, None),
            P("section", "pool", None, None, "tp", None, None),
            P("section", "pool", None),
            P("section", "pool", None, None),
            P(),
            P(),
            P("section", "tp", None),
            P(("section", "pool"), None, "tp"),
            P(("section", "pool"), None, "tp"),
        ),
        out_specs=P("section", "pool", None, "tp"),
        check_vma=False,
    )
```

time: 204 us -> 128 us (0.63)
  blocking collectives: 73.9 us -> 0 us
  Pallas kernels: 0 us -> 48.9 us
  matrix products: 39.6 us -> 0 us
  starting transfers between devices: 0.3 us -> 29.5 us
  other arithmetic: 25.9 us -> 3.21 us
  between operations: 15 us -> 0.27 us
  local copies, waits for them, and re-layouts: 17.2 us -> 2.7 us
  waiting for transfers between devices: 31.7 us -> 43.1 us
    pallas_call x0 -> x10, Pallas kernels: none -> 48.9 us  [the longest x4 19.6 us: project(): pl.pallas_call(project_kernel, in_specs=[pl.BlockSpec(memory_space=pltpu....]
    all_to_all x1 -> x0, blocking collectives: 45.5 us -> none  [per_device(): lax.all_to_all(product.astype(jnp.bfloat16), 'pool', split_axis=0, concat...]
    ppermute x1 -> x25, waiting for transfers between devices: 1.9 us -> 43.1 us  [the longest x4 17.2 us: project_piece(): arrived.append(lax.ppermute(piece, ('section', 'tp'), pairs))]
    dot_general x4 -> x0, matrix products: 31.4 us -> none  [the longest x1 17.5 us: per_device(): partial_out = jnp.dot(flat_rows, wo[0], preferred_element_type=jnp.float32)]
    all_gather x1 -> x0, waiting for transfers between devices: 29.7 us -> none  [per_device(): everyone = lax.all_gather(context, 'pool', axis=0, tiled=True)]
    ppermute x1 -> x25, starting transfers between devices: 0.07 us -> 29.5 us  [the longest x6 13.3 us: gather(): return lax.ppermute(value, 'pool', ring)]
    psum x1 -> x0, blocking collectives: 28.4 us -> none  [per_device(): rank_hidden = lax.psum(rank_hidden, 'tp')]
    select_n x3 -> x0, other arithmetic: 15 us -> none  [the longest x2 15 us: attend(): picked = jnp.take(cache_pages, page_rows, axis=0)]
  transfers between devices with their start and end apart: 3 -> 25, of which waited for: 2 -> 15; matrix products, arithmetic and copies ran while one was open for 13% -> 2% of each run, Pallas kernels for 0% -> 30%
where the time goes in v1:
time: 128 us
  Pallas kernels  48.9 us (38%)
  waiting for transfers between devices  43.1 us (34%)
  starting transfers between devices  29.5 us (23%)
  other arithmetic  3.21 us (3%)
  local copies, waits for them, and re-layouts  2.7 us (2%)
    pallas_call x4, Pallas kernels, project(): pl.pallas_call(project_kernel, in_specs=[pl.BlockSpec(memory_space=pltpu....  19.6 us
    ppermute x4, waiting for transfers between devices, project_piece(): arrived.append(lax.ppermute(piece, ('section', 'tp'), pairs))  17.2 us
    pallas_call x2, Pallas kernels, attend(): pl.pallas_call(functools.partial(attend_kernel, first), grid=(1,), in_spe...  16.2 us
    ppermute x6, starting transfers between devices, gather(): return lax.ppermute(value, 'pool', ring)  13.3 us
    pallas_call x4, Pallas kernels, small_call(): pl.pallas_call(kernel, grid=(1,), in_specs=[smem] * 3 + [whole(weights)]...  13.1 us
    ppermute x2, waiting for transfers between devices, scatter(): return lax.ppermute(value, ('section', 'pool'), ring_next)  7.15 us
    ppermute x6, waiting for transfers between devices, up_of(): ranks.append(lax.ppermute(mine, 'tp', pairs))  7.15 us
    ppermute x6, starting transfers between devices, up_of(): ranks.append(lax.ppermute(mine, 'tp', pairs))  6.98 us
  transfers between devices with their start and end apart: 25, of which 15 were waited for; matrix products, arithmetic and copies ran while one was open for 2% of the time, Pallas kernels for 30%

profile of v1, /device:TPU:0, one launch (start us, length us, event | category | flops | bytes accessed | tf_op | source)
XLA Modules:
  0.0 127.7 jit_solution(17821795460089592564)
XLA Ops:
  0.0 8.1 %attend.2.refs_0_ = bf16[64,2048]{1,0:T(8,128)(2,1)} custom-call(s32[16]{0:T(128)} %bitcast.29, s32[16,16]{1,0:T(8,128)} %bitcast.27, bf16[16,128,128]{2,1,0:T(8,128)(2,1)} %bitcast.23, bf16[16,2,2,8,128]{4,3,2,1,0:T(8,128)(2,1)} %bitcast.25, bf16[128,2,2,64,128]{4,3,2,1,0:T(8,128)(2,1)} %bitcast.21), custom_call_target="tpu_custom_call" | custom-call | flops 500000000 | bytes 12000000 | tf_op jit(solution)/shard_map/attend/pallas_call | solution.py:180
  8.1 4.9 %collective-permute-start.1 = (bf16[64,2048]{1,0:T(8,128)(2,1)}, bf16[64,2048]{1,0:T(8,128)(2,1)S(1)}, u32[]{:S(2)}, u32[]{:S(2)}) collective-permute-start(bf16[64,2048]{1,0:T(8,128)(2,1)} %attend.2.refs_0_), channel_id=1, source_target_pairs={{0,2},{2,3},{3,1},{1,0},{4,6},{6,7},{7,5},{5,4},{8,10},{10,11},{11... | collective-permute-start | bytes 786440 | tf_op jit(solution)/shard_map/ppermute | solution.py:414
  12.9 5.9 %collective-permute-done.1.refs_1_ = bf16[64,2048]{1,0:T(8,128)(2,1)S(1)} collective-permute-done((bf16[64,2048]{1,0:T(8,128)(2,1)}, bf16[64,2048]{1,0:T(8,128)(2,1)S(1)}, u32[]{:S(2)}, u32[]{:S(2)}) %collective-permute-start.1) | collective-permute-done | bytes 262176 | tf_op jit(solution)/shard_map/ppermute | solution.py:414
  18.9 3.3 %collective-permute-start.3 = (bf16[64,2048]{1,0:T(8,128)(2,1)S(1)}, bf16[64,2048]{1,0:T(8,128)(2,1)S(1)}, u32[]{:S(2)}, u32[]{:S(2)}) collective-permute-start(bf16[64,2048]{1,0:T(8,128)(2,1)S(1)} %collective-permute-done.1.refs_1_), channel_id=1, source_target_pairs={{0,2},{2,3},{3,1},{1,0},{4,6},{6,7},{7,5},{5,4},{8,10},{10,11},{11... | collective-permute-start | bytes 786440 | tf_op jit(solution)/shard_map/ppermute | solution.py:414
  22.1 8.2 %attend.3.refs_1_.refs_0_ = bf16[64,2048]{1,0:T(8,128)(2,1)} custom-call(s32[16]{0:T(128)} %bitcast.30, s32[16,16]{1,0:T(8,128)} %bitcast.28, bf16[16,128,128]{2,1,0:T(8,128)(2,1)} %bitcast.24, bf16[16,2,2,8,128]{4,3,2,1,0:T(8,128)(2,1)} %bitcast.26, bf16[128,2,2,64,128]{4,3,2,1,0:T(8,128)(2,1)} %bitcast.22), custom_call_target="tpu_custom_call" | custom-call | flops 500000000 | bytes 12000000 | tf_op jit(solution)/shard_map/attend/pallas_call | solution.py:180
  30.3 0.8 collective-permute-start.5
  31.1 4.9 %project.4 = bf16[128,2048]{1,0:T(8,128)(2,1)} custom-call(s32[1]{0:T(128)} %bitcast.1.piece, bf16[64,2048]{1,0:T(8,128)(2,1)} %attend.2.refs_0_, bf16[64,2048]{1,0:T(8,128)(2,1)} %attend.3.refs_1_.refs_0_, bf16[2048,8192]{1,0:T(8,128)(2,1)} %bitcast.17), custom_call_target="tpu_custom_call" | custom-call | flops 1073741824 | bytes 9437184 | tf_op jit(solution)/shard_map/project/pallas_call | solution.py:254
  36.0 1.2 collective-permute-start.7
  37.2 4.9 %project.5 = bf16[128,2048]{1,0:T(8,128)(2,1)} custom-call(s32[1]{0:T(128)} %bitcast.10.piece, bf16[64,2048]{1,0:T(8,128)(2,1)} %attend.2.refs_0_, bf16[64,2048]{1,0:T(8,128)(2,1)} %attend.3.refs_1_.refs_0_, bf16[2048,8192]{1,0:T(8,128)(2,1)} %bitcast.18), custom_call_target="tpu_custom_call" | custom-call | flops 1073741824 | bytes 9437184 | tf_op jit(solution)/shard_map/project/pallas_call | solution.py:254
  42.1 0.0 copy-start.3
  42.1 1.0 collective-permute-start.8
  43.1 0.6 pad_add_fusion.where
  43.7 4.9 %project.6 = bf16[128,2048]{1,0:T(8,128)(2,1)} custom-call(s32[1]{0:T(128)} %bitcast.11.piece, bf16[64,2048]{1,0:T(8,128)(2,1)} %attend.2.refs_0_, bf16[64,2048]{1,0:T(8,128)(2,1)} %attend.3.refs_1_.refs_0_, bf16[2048,8192]{1,0:T(8,128)(2,1)} %bitcast.19), custom_call_target="tpu_custom_call" | custom-call | flops 1073741824 | bytes 9437184 | tf_op jit(solution)/shard_map/project/pallas_call | solution.py:254
  48.6 0.0 collective-permute-done.7.refs_3_
  48.6 0.7 copy-done.11
  49.3 3.2 %shard_map.109.refs_0_ = bf16[256,128]{1,0:T(8,128)(2,1)} custom-call(s32[2]{0:T(128)} %pad_add_fusion.where, s32[2,4,16]{2,1,0:T(4,128)} %adapters_of.7, s32[64]{0:T(128)} %slot_of.7, bf16[8,64,2048]{2,1,0:T(8,128)(2,1)} %down.3, bf16[64,2048]{1,0:T(8,128)(2,1)} %attend.2.refs_0_, bf16[64,2048]{1,0:T(8,128)(2,1)} %copy-done.5, bf16[64,2048]{1,0:T(8,128)(2,1)} %copy-done.7, ...), custom_call_target="tpu_custom_call" | custom-call | flops 536870912 | bytes 3145728 | tf_op jit(solution)/shard_map/pallas_call | solution.py:353
  52.5 0.0 collective-permute-done.8.refs_2_
  52.5 2.2 %collective-permute-start.12 = (bf16[64,2048]{1,0:T(8,128)(2,1)S(1)}, bf16[64,2048]{1,0:T(8,128)(2,1)S(1)}, u32[]{:S(2)}, u32[]{:S(2)}) collective-permute-start(bf16[64,2048]{1,0:T(8,128)(2,1)S(1)} %collective-permute-done.8.refs_2_), channel_id=1, source_target_pairs={{0,2},{2,3},{3,1},{1,0},{4,6},{6,7},{7,5},{5,4},{8,10},{10,11},{11... | collective-permute-start | bytes 786440 | tf_op jit(solution)/shard_map/ppermute | solution.py:414
  54.7 1.5 %collective-permute-start.10 = (bf16[256,128]{1,0:T(8,128)(2,1)}, bf16[256,128]{1,0:T(8,128)(2,1)S(1)}, u32[]{:S(2)}, u32[]{:S(2)}) collective-permute-start(bf16[256,128]{1,0:T(8,128)(2,1)} %shard_map.109.refs_0_), channel_id=1, source_target_pairs={{0,8},{4,12},{8,0},{12,4},{1,9},{5,13},{9,1},{13,5},{2,10},{6,14},... | collective-permute-start | bytes 196616 | tf_op jit(solution)/shard_map/ppermute | solution.py:449
  56.2 1.5 %collective-permute-start.11 = (bf16[256,128]{1,0:T(8,128)(2,1)}, bf16[256,128]{1,0:T(8,128)(2,1)S(1)}, u32[]{:S(2)}, u32[]{:S(2)}) collective-permute-start(bf16[256,128]{1,0:T(8,128)(2,1)} %shard_map.109.refs_0_), channel_id=1, source_target_pairs={{0,4},{4,0},{8,12},{12,8},{1,5},{5,1},{9,13},{13,9},{2,6},{6,2},{1... | collective-permute-start | bytes 196616 | tf_op jit(solution)/shard_map/ppermute | solution.py:449
  57.7 0.5 collective-permute-start.9
  58.2 1.6 %collective-permute-done.10.refs_2_ = bf16[256,128]{1,0:T(8,128)(2,1)S(1)} collective-permute-done((bf16[256,128]{1,0:T(8,128)(2,1)}, bf16[256,128]{1,0:T(8,128)(2,1)S(1)}, u32[]{:S(2)}, u32[]{:S(2)}) %collective-permute-start.10) | collective-permute-done | bytes 65568 | tf_op jit(solution)/shard_map/ppermute | solution.py:449
  59.8 0.9 collective-permute-done.11.refs_3_
  60.7 2.4 %collective-permute-done.9.refs_1_ = bf16[256,128]{1,0:T(8,128)(2,1)S(1)} collective-permute-done((bf16[256,128]{1,0:T(8,128)(2,1)}, bf16[256,128]{1,0:T(8,128)(2,1)S(1)}, u32[]{:S(2)}, u32[]{:S(2)}) %collective-permute-start.9) | collective-permute-done | bytes 65568 | tf_op jit(solution)/shard_map/ppermute | solution.py:449
  63.1 0.6 copy-done.17
  63.8 3.3 %shard_map.110 = (bf16[64,2048]{1,0:T(8,128)(2,1)}, bf16[64,2048]{1,0:T(8,128)(2,1)}, bf16[64,2048]{1,0:T(8,128)(2,1)}, bf16[64,2048]{1,0:T(8,128)(2,1)}) custom-call(s32[2]{0:T(128)} %pad_add_fusion.where, s32[2,4,16]{2,1,0:T(4,128)} %adapters_of.7, s32[64]{0:T(128)} %slot_of.7, bf16[8,64,2048]{2,1,0:T(8,128)(2,1)} %up.3, ...), custom_call_target="tpu_custom_call" | custom-call | flops 536870912 | bytes 2359296 | tf_op jit(solution)/shard_map/pallas_call | solution.py:353
  67.1 0.0 collective-permute-done.12.refs_3_
  67.1 0.7 copy-done.9
  67.8 3.2 %shard_map.111.refs_0_ = bf16[256,128]{1,0:T(8,128)(2,1)} custom-call(s32[2]{0:T(128)} %pad_add_fusion.where, s32[2,4,16]{2,1,0:T(4,128)} %adapters_of.7, s32[64]{0:T(128)} %slot_of.7, bf16[8,64,2048]{2,1,0:T(8,128)(2,1)} %down.3, bf16[64,2048]{1,0:T(8,128)(2,1)} %attend.3.refs_1_.refs_0_, bf16[64,2048]{1,0:T(8,128)(2,1)} %copy-done.3, ...), custom_call_target="tpu_custom_call" | custom-call | flops 536870912 | bytes 3145728 | tf_op jit(solution)/shard_map/pallas_call | solution.py:353
  71.0 0.7 collective-permute-start.13
  71.7 1.3 %collective-permute-start.14 = (bf16[256,128]{1,0:T(8,128)(2,1)}, bf16[256,128]{1,0:T(8,128)(2,1)S(1)}, u32[]{:S(2)}, u32[]{:S(2)}) collective-permute-start(bf16[256,128]{1,0:T(8,128)(2,1)} %shard_map.111.refs_0_), channel_id=1, source_target_pairs={{0,8},{4,12},{8,0},{12,4},{1,9},{5,13},{9,1},{13,5},{2,10},{6,14},... | collective-permute-start | bytes 196616 | tf_op jit(solution)/shard_map/ppermute | solution.py:449
  73.0 1.5 %collective-permute-start.15 = (bf16[256,128]{1,0:T(8,128)(2,1)}, bf16[256,128]{1,0:T(8,128)(2,1)S(1)}, u32[]{:S(2)}, u32[]{:S(2)}) collective-permute-start(bf16[256,128]{1,0:T(8,128)(2,1)} %shard_map.111.refs_0_), channel_id=1, source_target_pairs={{0,4},{4,0},{8,12},{12,8},{1,5},{5,1},{9,13},{13,9},{2,6},{6,2},{1... | collective-permute-start | bytes 196616 | tf_op jit(solution)/shard_map/ppermute | solution.py:449
  74.5 0.7 collective-permute-start.18
  75.2 1.3 collective-permute-done.13.refs_1_
  76.5 0.4 collective-permute-done.14.refs_2_
  76.9 0.6 collective-permute-done.15.refs_3_
  77.5 0.0 copy-done.13
  77.5 0.6 copy-done.15
  78.1 3.3 %shard_map.112 = (bf16[64,2048]{1,0:T(8,128)(2,1)}, bf16[64,2048]{1,0:T(8,128)(2,1)}, bf16[64,2048]{1,0:T(8,128)(2,1)}, bf16[64,2048]{1,0:T(8,128)(2,1)}) custom-call(s32[2]{0:T(128)} %pad_add_fusion.where, s32[2,4,16]{2,1,0:T(4,128)} %adapters_of.7, s32[64]{0:T(128)} %slot_of.7, bf16[8,64,2048]{2,1,0:T(8,128)(2,1)} %up.3, ...), custom_call_target="tpu_custom_call" | custom-call | flops 536870912 | bytes 2359296 | tf_op jit(solution)/shard_map/pallas_call | solution.py:353
  81.4 0.7 collective-permute-start.22
  82.2 1.0 collective-permute-done.18
  83.2 1.0 add.37
  84.2 1.6 %collective-permute-start.19 = (bf16[64,2048]{1,0:T(8,128)(2,1)S(1)}, bf16[64,2048]{1,0:T(8,128)(2,1)S(1)}, u32[]{:S(2)}, u32[]{:S(2)}) collective-permute-start(bf16[64,2048]{1,0:T(8,128)(2,1)S(1)} %add.37), channel_id=1, source_target_pairs={{0,2},{2,3},{3,1},{1,0},{4,6},{6,7},{7,5},{5,4},{8,10},{10,11},{11... | collective-permute-start | bytes 786440 | tf_op jit(solution)/shard_map/ppermute | solution.py:465
  85.9 5.0 %project.7 = bf16[128,2048]{1,0:T(8,128)(2,1)} custom-call(s32[1]{0:T(128)} %bitcast.12.piece, bf16[64,2048]{1,0:T(8,128)(2,1)} %attend.2.refs_0_, bf16[64,2048]{1,0:T(8,128)(2,1)} %attend.3.refs_1_.refs_0_, bf16[2048,8192]{1,0:T(8,128)(2,1)} %bitcast.20), custom_call_target="tpu_custom_call" | custom-call | flops 1073741824 | bytes 9437184 | tf_op jit(solution)/shard_map/project/pallas_call | solution.py:254
  90.9 0.1 add.40
  91.0 1.6 %collective-permute-start.23 = (bf16[64,2048]{1,0:T(8,128)(2,1)S(1)}, bf16[64,2048]{1,0:T(8,128)(2,1)S(1)}, u32[]{:S(2)}, u32[]{:S(2)}) collective-permute-start(bf16[64,2048]{1,0:T(8,128)(2,1)S(1)} %add.40), channel_id=1, source_target_pairs={{0,2},{2,3},{3,1},{1,0},{4,6},{6,7},{7,5},{5,4},{8,10},{10,11},{11... | collective-permute-start | bytes 786440 | tf_op jit(solution)/shard_map/ppermute | solution.py:465
  92.6 0.5 collective-permute-start.21
  93.1 2.0 %collective-permute-done.19 = bf16[64,2048]{1,0:T(8,128)(2,1)S(1)} collective-permute-done((bf16[64,2048]{1,0:T(8,128)(2,1)S(1)}, bf16[64,2048]{1,0:T(8,128)(2,1)S(1)}, u32[]{:S(2)}, u32[]{:S(2)}) %collective-permute-start.19) | collective-permute-done | bytes 262176 | tf_op jit(solution)/shard_map/ppermute | solution.py:465
  95.1 0.1 add.38
  95.2 0.1 collective-permute-start.20
  95.2 2.7 %collective-permute-done.23 = bf16[64,2048]{1,0:T(8,128)(2,1)S(1)} collective-permute-done((bf16[64,2048]{1,0:T(8,128)(2,1)S(1)}, bf16[64,2048]{1,0:T(8,128)(2,1)S(1)}, u32[]{:S(2)}, u32[]{:S(2)}) %collective-permute-start.23) | collective-permute-done | bytes 262176 | tf_op jit(solution)/shard_map/ppermute | solution.py:465
  97.9 0.1 add.41
  98.0 0.1 collective-permute-start.24
  98.1 2.0 %collective-permute-start = (bf16[128,2048]{1,0:T(8,128)(2,1)}, bf16[128,2048]{1,0:T(8,128)(2,1)S(1)}, u32[]{:S(2)}, u32[]{:S(2)}) collective-permute-start(bf16[128,2048]{1,0:T(8,128)(2,1)} %bitcast.31), channel_id=1, source_target_pairs={{0,16},{16,0},{1,17},{17,1},{2,18},{18,2},{3,19},{19,3},{4,20},{20... | collective-permute-start | bytes 1572872 | tf_op jit(solution)/shard_map/ppermute | solution.py:467
  100.1 0.5 collective-permute-start.2
  100.6 1.4 %collective-permute-start.6 = (bf16[128,2048]{1,0:T(8,128)(2,1)S(1)}, bf16[128,2048]{1,0:T(8,128)(2,1)S(1)}, u32[]{:S(2)}, u32[]{:S(2)}) collective-permute-start(bf16[128,2048]{1,0:T(8,128)(2,1)S(1)} %copy-done.2), channel_id=1, source_target_pairs={{0,20},{4,16},{8,28},{12,24},{16,4},{20,0},{24,12},{28,8},{1,21},{... | collective-permute-start | bytes 1572872 | tf_op jit(solution)/shard_map/ppermute | solution.py:427
  102.0 1.8 %collective-permute-done.20 = bf16[64,2048]{1,0:T(8,128)(2,1)S(1)} collective-permute-done((bf16[64,2048]{1,0:T(8,128)(2,1)S(1)}, bf16[64,2048]{1,0:T(8,128)(2,1)S(1)}, u32[]{:S(2)}, u32[]{:S(2)}) %collective-permute-start.20) | collective-permute-done | bytes 262176 | tf_op jit(solution)/shard_map/ppermute | solution.py:464
  103.8 5.3 %collective-permute-done.24 = bf16[64,2048]{1,0:T(8,128)(2,1)S(1)} collective-permute-done((bf16[64,2048]{1,0:T(8,128)(2,1)S(1)}, bf16[64,2048]{1,0:T(8,128)(2,1)S(1)}, u32[]{:S(2)}, u32[]{:S(2)}) %collective-permute-start.24) | collective-permute-done | bytes 262176 | tf_op jit(solution)/shard_map/ppermute | solution.py:464
  109.2 0.1 convert_add_fusion.1
  109.2 0.1 convert_add_fusion
  109.3 5.8 %collective-permute-done.2 = bf16[128,2048]{1,0:T(8,128)(2,1)S(1)} collective-permute-done((bf16[128,2048]{1,0:T(8,128)(2,1)S(1)}, bf16[128,2048]{1,0:T(8,128)(2,1)S(1)}, u32[]{:S(2)}, u32[]{:S(2)}) %collective-permute-start.2) | collective-permute-done | bytes 524320 | tf_op jit(solution)/shard_map/ppermute | solution.py:427
  115.1 10.4 %collective-permute-done.6 = bf16[128,2048]{1,0:T(8,128)(2,1)S(1)} collective-permute-done((bf16[128,2048]{1,0:T(8,128)(2,1)S(1)}, bf16[128,2048]{1,0:T(8,128)(2,1)S(1)}, u32[]{:S(2)}, u32[]{:S(2)}) %collective-permute-start.6) | collective-permute-done | bytes 524320 | tf_op jit(solution)/shard_map/ppermute | solution.py:427
  125.5 1.0 collective-permute-done.4
  126.4 1.3 fusion.1
  (42 shorter events, 0.1 us)
Async XLA Ops:
  8.1 10.8 %collective-permute-start.1 = (bf16[64,2048]{1,0:T(8,128)(2,1)}, bf16[64,2048]{1,0:T(8,128)(2,1)S(1)}, u32[]{:S(2)}, u32[]{:S(2)}) collective-permute-start(bf16[64,2048]{1,0:T(8,128)(2,1)} %attend.2.refs_0_), channel_id=1, source_target_pairs={{0,2},{2,3},{3,1},{1,0},{4,6},{6,7},{7,5},{5,4},{8,10},{10,11},{11... | collective-permute-start | bytes 786440 | tf_op jit(solution)/shard_map/ppermute | solution.py:414
  18.9 17.1 %copy-start.5 = (bf16[64,2048]{1,0:T(8,128)(2,1)}, bf16[64,2048]{1,0:T(8,128)(2,1)S(1)}, u32[]{:S(2)}) copy-start(bf16[64,2048]{1,0:T(8,128)(2,1)S(1)} %collective-permute-done.1.refs_1_) | copy-start | bytes 786436
  18.9 17.2 %collective-permute-start.3 = (bf16[64,2048]{1,0:T(8,128)(2,1)S(1)}, bf16[64,2048]{1,0:T(8,128)(2,1)S(1)}, u32[]{:S(2)}, u32[]{:S(2)}) collective-permute-start(bf16[64,2048]{1,0:T(8,128)(2,1)S(1)} %collective-permute-done.1.refs_1_), channel_id=1, source_target_pairs={{0,2},{2,3},{3,1},{1,0},{4,6},{6,7},{7,5},{5,4},{8,10},{10,11},{11... | collective-permute-start | bytes 786440 | tf_op jit(solution)/shard_map/ppermute | solution.py:414
  30.3 11.8 %collective-permute-start.5 = (bf16[64,2048]{1,0:T(8,128)(2,1)}, bf16[64,2048]{1,0:T(8,128)(2,1)S(1)}, u32[]{:S(2)}, u32[]{:S(2)}) collective-permute-start(bf16[64,2048]{1,0:T(8,128)(2,1)} %attend.3.refs_1_.refs_0_), channel_id=1, source_target_pairs={{0,2},{2,3},{3,1},{1,0},{4,6},{6,7},{7,5},{5,4},{8,10},{10,11},{11... | collective-permute-start | bytes 786440 | tf_op jit(solution)/shard_map/ppermute | solution.py:414
  36.0 6.1 %copy-start.7 = (bf16[64,2048]{1,0:T(8,128)(2,1)}, bf16[64,2048]{1,0:T(8,128)(2,1)S(1)}, u32[]{:S(2)}) copy-start(bf16[64,2048]{1,0:T(8,128)(2,1)S(1)} %collective-permute-done.3.refs_2_) | copy-start | bytes 786436
  36.0 12.6 %collective-permute-start.7 = (bf16[64,2048]{1,0:T(8,128)(2,1)S(1)}, bf16[64,2048]{1,0:T(8,128)(2,1)S(1)}, u32[]{:S(2)}, u32[]{:S(2)}) collective-permute-start(bf16[64,2048]{1,0:T(8,128)(2,1)S(1)} %collective-permute-done.3.refs_2_), channel_id=1, source_target_pairs={{0,2},{2,3},{3,1},{1,0},{4,6},{6,7},{7,5},{5,4},{8,10},{10,11},{11... | collective-permute-start | bytes 786440 | tf_op jit(solution)/shard_map/ppermute | solution.py:414
  42.1 6.5 %copy-start.3 = (bf16[64,2048]{1,0:T(8,128)(2,1)}, bf16[64,2048]{1,0:T(8,128)(2,1)S(1)}, u32[]{:S(2)}) copy-start(bf16[64,2048]{1,0:T(8,128)(2,1)S(1)} %collective-permute-done.5.refs_1_) | copy-start | bytes 786436
  42.1 10.4 %collective-permute-start.8 = (bf16[64,2048]{1,0:T(8,128)(2,1)S(1)}, bf16[64,2048]{1,0:T(8,128)(2,1)S(1)}, u32[]{:S(2)}, u32[]{:S(2)}) collective-permute-start(bf16[64,2048]{1,0:T(8,128)(2,1)S(1)} %collective-permute-done.5.refs_1_), channel_id=1, source_target_pairs={{0,2},{2,3},{3,1},{1,0},{4,6},{6,7},{7,5},{5,4},{8,10},{10,11},{11... | collective-permute-start | bytes 786440 | tf_op jit(solution)/shard_map/ppermute | solution.py:414
  48.6 0.7 copy-start.11
  52.5 14.6 %copy-start.8 = (bf16[64,2048]{1,0:T(8,128)(2,1)}, bf16[64,2048]{1,0:T(8,128)(2,1)S(1)}, u32[]{:S(2)}) copy-start(bf16[64,2048]{1,0:T(8,128)(2,1)S(1)} %collective-permute-done.8.refs_2_) | copy-start | bytes 786436
  52.5 14.6 %collective-permute-start.12 = (bf16[64,2048]{1,0:T(8,128)(2,1)S(1)}, bf16[64,2048]{1,0:T(8,128)(2,1)S(1)}, u32[]{:S(2)}, u32[]{:S(2)}) collective-permute-start(bf16[64,2048]{1,0:T(8,128)(2,1)S(1)} %collective-permute-done.8.refs_2_), channel_id=1, source_target_pairs={{0,2},{2,3},{3,1},{1,0},{4,6},{6,7},{7,5},{5,4},{8,10},{10,11},{11... | collective-permute-start | bytes 786440 | tf_op jit(solution)/shard_map/ppermute | solution.py:414
  54.7 5.1 %collective-permute-start.10 = (bf16[256,128]{1,0:T(8,128)(2,1)}, bf16[256,128]{1,0:T(8,128)(2,1)S(1)}, u32[]{:S(2)}, u32[]{:S(2)}) collective-permute-start(bf16[256,128]{1,0:T(8,128)(2,1)} %shard_map.109.refs_0_), channel_id=1, source_target_pairs={{0,8},{4,12},{8,0},{12,4},{1,9},{5,13},{9,1},{13,5},{2,10},{6,14},... | collective-permute-start | bytes 196616 | tf_op jit(solution)/shard_map/ppermute | solution.py:449
  56.2 4.5 %collective-permute-start.11 = (bf16[256,128]{1,0:T(8,128)(2,1)}, bf16[256,128]{1,0:T(8,128)(2,1)S(1)}, u32[]{:S(2)}, u32[]{:S(2)}) collective-permute-start(bf16[256,128]{1,0:T(8,128)(2,1)} %shard_map.109.refs_0_), channel_id=1, source_target_pairs={{0,4},{4,0},{8,12},{12,8},{1,5},{5,1},{9,13},{13,9},{2,6},{6,2},{1... | collective-permute-start | bytes 196616 | tf_op jit(solution)/shard_map/ppermute | solution.py:449
  57.7 5.4 %collective-permute-start.9 = (bf16[256,128]{1,0:T(8,128)(2,1)}, bf16[256,128]{1,0:T(8,128)(2,1)S(1)}, u32[]{:S(2)}, u32[]{:S(2)}) collective-permute-start(bf16[256,128]{1,0:T(8,128)(2,1)} %shard_map.109.refs_0_), channel_id=1, source_target_pairs={{0,12},{4,8},{8,4},{12,0},{1,13},{5,9},{9,5},{13,1},{2,14},{6,10},... | collective-permute-start | bytes 196616 | tf_op jit(solution)/shard_map/ppermute | solution.py:449
  59.8 3.3 %copy-start.14 = (bf16[256,128]{1,0:T(8,128)(2,1)}, bf16[256,128]{1,0:T(8,128)(2,1)S(1)}, u32[]{:S(2)}) copy-start(bf16[256,128]{1,0:T(8,128)(2,1)S(1)} %collective-permute-done.10.refs_2_) | copy-start | bytes 196612
  60.7 2.4 %copy-start.16 = (bf16[256,128]{1,0:T(8,128)(2,1)}, bf16[256,128]{1,0:T(8,128)(2,1)S(1)}, u32[]{:S(2)}) copy-start(bf16[256,128]{1,0:T(8,128)(2,1)S(1)} %collective-permute-done.11.refs_3_) | copy-start | bytes 196612
  63.1 0.6 copy-start.17
  67.1 0.7 copy-start.9
  71.0 5.5 %collective-permute-start.13 = (bf16[256,128]{1,0:T(8,128)(2,1)}, bf16[256,128]{1,0:T(8,128)(2,1)S(1)}, u32[]{:S(2)}, u32[]{:S(2)}) collective-permute-start(bf16[256,128]{1,0:T(8,128)(2,1)} %shard_map.111.refs_0_), channel_id=1, source_target_pairs={{0,12},{4,8},{8,4},{12,0},{1,13},{5,9},{9,5},{13,1},{2,14},{6,10},... | collective-permute-start | bytes 196616 | tf_op jit(solution)/shard_map/ppermute | solution.py:449
  71.7 5.2 %collective-permute-start.14 = (bf16[256,128]{1,0:T(8,128)(2,1)}, bf16[256,128]{1,0:T(8,128)(2,1)S(1)}, u32[]{:S(2)}, u32[]{:S(2)}) collective-permute-start(bf16[256,128]{1,0:T(8,128)(2,1)} %shard_map.111.refs_0_), channel_id=1, source_target_pairs={{0,8},{4,12},{8,0},{12,4},{1,9},{5,13},{9,1},{13,5},{2,10},{6,14},... | collective-permute-start | bytes 196616 | tf_op jit(solution)/shard_map/ppermute | solution.py:449
  73.0 4.5 %collective-permute-start.15 = (bf16[256,128]{1,0:T(8,128)(2,1)}, bf16[256,128]{1,0:T(8,128)(2,1)S(1)}, u32[]{:S(2)}, u32[]{:S(2)}) collective-permute-start(bf16[256,128]{1,0:T(8,128)(2,1)} %shard_map.111.refs_0_), channel_id=1, source_target_pairs={{0,4},{4,0},{8,12},{12,8},{1,5},{5,1},{9,13},{13,9},{2,6},{6,2},{1... | collective-permute-start | bytes 196616 | tf_op jit(solution)/shard_map/ppermute | solution.py:449
  74.5 8.7 %collective-permute-start.18 = (bf16[64,2048]{1,0:T(8,128)(2,1)}, bf16[64,2048]{1,0:T(8,128)(2,1)S(1)}, u32[]{:S(2)}, u32[]{:S(2)}) collective-permute-start(bf16[64,2048]{1,0:T(8,128)(2,1)} %get-tuple-element.42), channel_id=1, source_target_pairs={{0,2},{2,3},{3,1},{1,0},{4,6},{6,7},{7,5},{5,4},{8,10},{10,11},{11... | collective-permute-start | bytes 786440 | tf_op jit(solution)/shard_map/ppermute | solution.py:465
  76.5 1.0 copy-start.12
  76.9 0.6 copy-start.13
  77.5 0.6 copy-start.15
  81.4 9.5 %collective-permute-start.22 = (bf16[64,2048]{1,0:T(8,128)(2,1)}, bf16[64,2048]{1,0:T(8,128)(2,1)S(1)}, u32[]{:S(2)}, u32[]{:S(2)}) collective-permute-start(bf16[64,2048]{1,0:T(8,128)(2,1)} %get-tuple-element.47), channel_id=1, source_target_pairs={{0,2},{2,3},{3,1},{1,0},{4,6},{6,7},{7,5},{5,4},{8,10},{10,11},{11... | collective-permute-start | bytes 786440 | tf_op jit(solution)/shard_map/ppermute | solution.py:465
  84.2 10.9 %collective-permute-start.19 = (bf16[64,2048]{1,0:T(8,128)(2,1)S(1)}, bf16[64,2048]{1,0:T(8,128)(2,1)S(1)}, u32[]{:S(2)}, u32[]{:S(2)}) collective-permute-start(bf16[64,2048]{1,0:T(8,128)(2,1)S(1)} %add.37), channel_id=1, source_target_pairs={{0,2},{2,3},{3,1},{1,0},{4,6},{6,7},{7,5},{5,4},{8,10},{10,11},{11... | collective-permute-start | bytes 786440 | tf_op jit(solution)/shard_map/ppermute | solution.py:465
  85.8 5.1 %copy-start.10 = (bf16[64,2048]{1,0:T(8,128)(2,1)S(1)}, bf16[64,2048]{1,0:T(8,128)(2,1)}, u32[]{:S(2)}) copy-start(bf16[64,2048]{1,0:T(8,128)(2,1)} %get-tuple-element.49) | copy-start | bytes 786436
  85.8 6.7 %copy-start.18 = (bf16[64,2048]{1,0:T(8,128)(2,1)S(1)}, bf16[64,2048]{1,0:T(8,128)(2,1)}, u32[]{:S(2)}) copy-start(bf16[64,2048]{1,0:T(8,128)(2,1)} %get-tuple-element.36) | copy-start | bytes 786436
  85.8 9.3 %copy-start.4 = (bf16[64,2048]{1,0:T(8,128)(2,1)S(1)}, bf16[64,2048]{1,0:T(8,128)(2,1)}, u32[]{:S(2)}) copy-start(bf16[64,2048]{1,0:T(8,128)(2,1)} %get-tuple-element.46) | copy-start | bytes 786436
  85.8 12.1 %copy-start.6 = (bf16[64,2048]{1,0:T(8,128)(2,1)S(1)}, bf16[64,2048]{1,0:T(8,128)(2,1)}, u32[]{:S(2)}) copy-start(bf16[64,2048]{1,0:T(8,128)(2,1)} %get-tuple-element.50) | copy-start | bytes 786436
  85.8 14.2 %copy-start = (bf16[128,2048]{1,0:T(8,128)(2,1)S(1)}, bf16[128,2048]{1,0:T(8,128)(2,1)}, u32[]{:S(2)}) copy-start(bf16[128,2048]{1,0:T(8,128)(2,1)} %project.4) | copy-start | bytes 1572868
  85.9 14.8 %copy-start.2 = (bf16[128,2048]{1,0:T(8,128)(2,1)S(1)}, bf16[128,2048]{1,0:T(8,128)(2,1)}, u32[]{:S(2)}) copy-start(bf16[128,2048]{1,0:T(8,128)(2,1)} %project.6) | copy-start | bytes 1572868
  85.9 18.0 %copy-start.1 = (bf16[128,2048]{1,0:T(8,128)(2,1)S(1)}, bf16[128,2048]{1,0:T(8,128)(2,1)}, u32[]{:S(2)}) copy-start(bf16[128,2048]{1,0:T(8,128)(2,1)} %project.5) | copy-start | bytes 1572868
  91.0 6.9 %collective-permute-start.23 = (bf16[64,2048]{1,0:T(8,128)(2,1)S(1)}, bf16[64,2048]{1,0:T(8,128)(2,1)S(1)}, u32[]{:S(2)}, u32[]{:S(2)}) collective-permute-start(bf16[64,2048]{1,0:T(8,128)(2,1)S(1)} %add.40), channel_id=1, source_target_pairs={{0,2},{2,3},{3,1},{1,0},{4,6},{6,7},{7,5},{5,4},{8,10},{10,11},{11... | collective-permute-start | bytes 786440 | tf_op jit(solution)/shard_map/ppermute | solution.py:465
  92.6 7.5 %collective-permute-start.17 = (bf16[64,2048]{1,0:T(8,128)(2,1)S(1)}, bf16[64,2048]{1,0:T(8,128)(2,1)S(1)}, u32[]{:S(2)}, u32[]{:S(2)}) collective-permute-start(bf16[64,2048]{1,0:T(8,128)(2,1)S(1)} %copy-done.18), channel_id=1, source_target_pairs={{0,16},{16,0},{1,17},{17,1},{2,18},{18,2},{3,19},{19,3},{4,20},{20... | collective-permute-start | bytes 786440 | tf_op jit(solution)/shard_map/ppermute | solution.py:487
  92.6 8.1 %collective-permute-start.21 = (bf16[64,2048]{1,0:T(8,128)(2,1)}, bf16[64,2048]{1,0:T(8,128)(2,1)S(1)}, u32[]{:S(2)}, u32[]{:S(2)}) collective-permute-start(bf16[64,2048]{1,0:T(8,128)(2,1)} %get-tuple-element.40), channel_id=1, source_target_pairs={{0,16},{16,0},{1,17},{17,1},{2,18},{18,2},{3,19},{19,3},{4,20},{20... | collective-permute-start | bytes 786440 | tf_op jit(solution)/shard_map/ppermute | solution.py:492
  95.2 8.7 %collective-permute-start.20 = (bf16[64,2048]{1,0:T(8,128)(2,1)S(1)}, bf16[64,2048]{1,0:T(8,128)(2,1)S(1)}, u32[]{:S(2)}, u32[]{:S(2)}) collective-permute-start(bf16[64,2048]{1,0:T(8,128)(2,1)S(1)} %add.38), channel_id=1, source_target_pairs={{0,18},{2,19},{3,17},{1,16},{16,2},{18,3},{19,1},{17,0},{4,22},{6,... | collective-permute-start | bytes 786440 | tf_op jit(solution)/shard_map/ppermute | solution.py:464
  98.0 11.2 %collective-permute-start.24 = (bf16[64,2048]{1,0:T(8,128)(2,1)S(1)}, bf16[64,2048]{1,0:T(8,128)(2,1)S(1)}, u32[]{:S(2)}, u32[]{:S(2)}) collective-permute-start(bf16[64,2048]{1,0:T(8,128)(2,1)S(1)} %add.41), channel_id=1, source_target_pairs={{0,18},{2,19},{3,17},{1,16},{16,2},{18,3},{19,1},{17,0},{4,22},{6,... | collective-permute-start | bytes 786440 | tf_op jit(solution)/shard_map/ppermute | solution.py:464
  98.1 11.2 %collective-permute-start = (bf16[128,2048]{1,0:T(8,128)(2,1)}, bf16[128,2048]{1,0:T(8,128)(2,1)S(1)}, u32[]{:S(2)}, u32[]{:S(2)}) collective-permute-start(bf16[128,2048]{1,0:T(8,128)(2,1)} %bitcast.31), channel_id=1, source_target_pairs={{0,16},{16,0},{1,17},{17,1},{2,18},{18,2},{3,19},{19,3},{4,20},{20... | collective-permute-start | bytes 1572872 | tf_op jit(solution)/shard_map/ppermute | solution.py:467
  100.1 15.0 %collective-permute-start.2 = (bf16[128,2048]{1,0:T(8,128)(2,1)S(1)}, bf16[128,2048]{1,0:T(8,128)(2,1)S(1)}, u32[]{:S(2)}, u32[]{:S(2)}) collective-permute-start(bf16[128,2048]{1,0:T(8,128)(2,1)S(1)} %copy-done), channel_id=1, source_target_pairs={{0,28},{4,24},{8,20},{12,16},{16,12},{20,8},{24,4},{28,0},{1,29},{... | collective-permute-start | bytes 1572872 | tf_op jit(solution)/shard_map/ppermute | solution.py:427
  100.6 24.9 %collective-permute-start.6 = (bf16[128,2048]{1,0:T(8,128)(2,1)S(1)}, bf16[128,2048]{1,0:T(8,128)(2,1)S(1)}, u32[]{:S(2)}, u32[]{:S(2)}) collective-permute-start(bf16[128,2048]{1,0:T(8,128)(2,1)S(1)} %copy-done.2), channel_id=1, source_target_pairs={{0,20},{4,16},{8,28},{12,24},{16,4},{20,0},{24,12},{28,8},{1,21},{... | collective-permute-start | bytes 1572872 | tf_op jit(solution)/shard_map/ppermute | solution.py:427
  103.8 22.6 %collective-permute-start.4 = (bf16[128,2048]{1,0:T(8,128)(2,1)S(1)}, bf16[128,2048]{1,0:T(8,128)(2,1)S(1)}, u32[]{:S(2)}, u32[]{:S(2)}) collective-permute-start(bf16[128,2048]{1,0:T(8,128)(2,1)S(1)} %copy-done.1), channel_id=1, source_target_pairs={{0,24},{4,28},{8,16},{12,20},{16,8},{20,12},{24,0},{28,4},{1,25},{... | collective-permute-start | bytes 1572872 | tf_op jit(solution)/shard_map/ppermute | solution.py:427
  109.2 17.3 %collective-permute-start.16 = (bf16[128,2048]{1,0:T(8,128)(2,1)}, bf16[128,2048]{1,0:T(8,128)(2,1)S(1)}, u32[]{:S(2)}, u32[]{:S(2)}) collective-permute-start(bf16[128,2048]{1,0:T(8,128)(2,1)} %project.7), channel_id=1, source_target_pairs={{0,16},{4,20},{8,24},{12,28},{16,0},{20,4},{24,8},{28,12},{1,17},{... | collective-permute-start | bytes 1572872 | tf_op jit(solution)/shard_map/ppermute | solution.py:427

commit v2 on v1

--- a/solution.py
+++ b/solution.py
@@ -188,7 +188,7 @@
             pl.BlockSpec(memory_space=pl.ANY),
         ],
         out_specs=pl.BlockSpec((requests * window_len, heads * head_size), lambda i: (0, 0)),
-        out_shape=jax.ShapeDtypeStruct((requests * window_len, heads * head_size), jnp.bfloat16),
+        out_shape=pltpu.VMEM((requests * window_len, heads * head_size), jnp.bfloat16),
         scratch_shapes=[
             pltpu.VMEM((requests, 2, kv_heads, max_keys, head_size), jnp.bfloat16),
             pltpu.SemaphoreType.DMA((requests, pages.shape[1])),
@@ -204,70 +204,69 @@
             pltpu.VMEM((ITEMS, kv_heads, rows, requests * window_len), jnp.bfloat16),
             pltpu.VMEM((ITEMS, kv_heads, rows, min(KEY_BLOCK, max_keys)), jnp.bfloat16),
         ],
+        compiler_params=room(
+            (requests, 2, kv_heads, max_keys, head_size),
+            (10, slots, kv_heads, rows, head_size),
+            (8, requests, rows_all, head_size),
+        ),
         cost_estimate=pl.CostEstimate(flops=500000000, bytes_accessed=12000000, transcendentals=0),
         name="attend",
-    )(lengths, pages, flat, window, cache)
-
-
-def project_kernel(piece, *refs):
-    count = len(refs) - 5
-    rows, weights, out = refs[:count], refs[count], refs[count + 1]
-    held, stored, sems = refs[count + 2 :]
+    )(lengths, pages, far(flat), far(window), far(cache))
+
+
+def project_kernel(count, extra, flip, *refs):
+    rows, weights, added = refs[:count], refs[count], refs[count + 1 : count + 1 + extra]
+    out, stored, sems = refs[count + 1 + extra :]
     blocks, _, block = stored.shape
-    each = held.shape[0] // count
-    start = piece[0] * (blocks * block)
-
-    def row_copy(i):
-        return pltpu.make_async_copy(
-            rows[i], held.at[pl.ds(i * each, each)], sems.at[blocks + i]
-        )
+    start = (lax.axis_index("tp") ^ flip) * (blocks * block)
 
     def weight_copy(b):
         at = pl.ds(pl.multiple_of(start + b * block, block), block)
         return pltpu.make_async_copy(weights.at[:, at], stored.at[b], sems.at[b])
 
-    for i in range(count):
-        row_copy(i).start()
     for b in range(blocks):
         weight_copy(b).start()
-    for i in range(count):
-        row_copy(i).wait()
 
     def step(b, carry):
         weight_copy(b).wait()
         at = pl.ds(pl.multiple_of(b * block, block), block)
-        out[:, at] = jnp.dot(
-            held[...], stored[b], preferred_element_type=jnp.float32
-        ).astype(out.dtype)
+        held = jnp.concatenate([r[...] for r in rows], axis=0)
+        made = jnp.dot(held, stored[b], preferred_element_type=jnp.float32)
+        if extra:
+            made = made + added[0][:, at].astype(jnp.float32)
+            made = made + jnp.concatenate([x[:, at] for x in added[1:]], axis=0).astype(jnp.float32)
+        out[:, at] = made.astype(out.dtype)
         return carry
 
     lax.fori_loop(0, blocks, step, 0)
 
 
-def project(chunks, weights, piece, pieces):
+def project(chunks, weights, flip, pieces, added=()):
     depth, width = weights.shape
     own = width // pieces
     block = min(256, own)
     blocks = own // block
     total = sum(c.shape[0] for c in chunks)
-    anywhere = pl.BlockSpec(memory_space=pl.ANY)
+    vmem = pl.BlockSpec(memory_space=pltpu.VMEM)
     return pl.pallas_call(
-        project_kernel,
-        in_specs=[pl.BlockSpec(memory_space=pltpu.SMEM)] + [anywhere] * (len(chunks) + 1),
-        out_specs=pl.BlockSpec(memory_space=pltpu.VMEM),
-        out_shape=jax.ShapeDtypeStruct((total, own), jnp.bfloat16),
+        functools.partial(project_kernel, len(chunks), len(added), flip),
+        in_specs=[vmem] * len(chunks)
+        + [pl.BlockSpec(memory_space=pl.ANY)]
+        + [vmem] * len(added),
+        out_specs=vmem,
+        out_shape=pltpu.VMEM((total, own), jnp.bfloat16),
         scratch_shapes=[
-            pltpu.VMEM((total, depth), jnp.bfloat16),
             pltpu.VMEM((blocks, depth, block), jnp.bfloat16),
-            pltpu.SemaphoreType.DMA((blocks + len(chunks),)),
+            pltpu.SemaphoreType.DMA((blocks,)),
         ],
+        compiler_params=room((depth, own), (2, total, depth)),
         cost_estimate=pl.CostEstimate(
             flops=2 * total * depth * own,
             bytes_accessed=2 * (depth * own + total * (depth + own)),
             transcendentals=0,
         ),
         name="project",
-    )(jnp.reshape(piece, (1,)).astype(jnp.int32), *chunks, weights)
+    )(*[near(c) for c in chunks], far(weights), *[near(x) for x in added])
 
 
 def pick(table, index):
@@ -277,8 +276,8 @@
     return value
 
 
-def local_slots(where, adapters_of, slot_of, order, steps, first, count, pages_here):
-    section, pool = where[0], where[1]
+def local_slots(section, pool, adapters_of, slot_of, order, steps, first, count, pages_here):
+    section, pool = section[0], pool[0]
     adapters = slot_of.shape[0] // adapters_of.shape[0]
     place_of = [order.index(p) for p in range(len(order))]
     place = pick(place_of, pool)
@@ -291,12 +290,14 @@
     return slots
 
 
-def rank_kernel(order, steps, first, count, where, adapters_of, slot_of, down, *refs):
+def rank_kernel(order, first, count, section, pool, adapters_of, slot_of, down, *refs):
     held, out = refs[:-1], refs[-1]
     pages_here, rank_width, features = down.shape
     wide_cols = pages_here * rank_width
     lanes = out.shape[1]
-    slots = local_slots(where, adapters_of, slot_of, order, steps, first, count, pages_here)
+    slots = local_slots(
+        section, pool, adapters_of, slot_of, order, range(len(order)), first, count, pages_here
+    )
     rows = jnp.concatenate([h[...] for h in held], axis=0)
     wide = lax.dot_general(
         rows, down[...].reshape(wide_cols, features), (((1,), (1,)), ((), ())),
@@ -311,19 +312,34 @@
         for start in range(lanes, wide_cols, lanes):
             total = total + kept[:, start : start + lanes]
         folded.append(total)
-    out[...] = jnp.concatenate(folded, axis=0).astype(out.dtype)
-
-
-def up_kernel(order, first, count, parts, where, adapters_of, slot_of, up, *refs):
+    total = jnp.concatenate(folded, axis=0)
+    both = total + pltpu.roll(total, rank_width, 1)
+    half = both.shape[0] // 2
+    lane = lax.broadcasted_iota(jnp.int32, (half, lanes), 1)
+    out[...] = jnp.where(lane < rank_width, both[:half], both[half:]).astype(out.dtype)
+
+
+def up_kernel(order, first, count, parts, section, pool, adapters_of, slot_of, up, *refs):
     ranks, outs = refs[:parts], refs[parts:]
     pages_here, rank_width, features = up.shape
     wide_cols = pages_here * rank_width
-    lanes = ranks[0].shape[1]
-    steps = range(len(order))
-    slots = local_slots(where, adapters_of, slot_of, order, steps, first, count, pages_here)
-    total = ranks[0][...].astype(jnp.float32)
+    each = outs[0].shape[0]
+    slots = local_slots(
+        section, pool, adapters_of, slot_of, order, range(len(order)), first, count, pages_here
+    )
+    packed = ranks[0][...].astype(jnp.float32)
     for other in ranks[1:]:
-        total = total + other[...].astype(jnp.float32)
+        packed = packed + other[...].astype(jnp.float32)
+    lanes = packed.shape[1]
+    turned = pltpu.roll(packed, rank_width, 1)
+    lane = lax.broadcasted_iota(jnp.int32, packed.shape, 1)
+    total = jnp.concatenate(
+        [
+            jnp.where(lane < rank_width, packed, turned),
+            jnp.where(lane < rank_width, turned, packed),
+        ],
+        axis=0,
+    )
     window_len = total.shape[0] // len(slots)
     page = lax.broadcasted_iota(jnp.int32, (window_len, wide_cols), 1) // rank_width
     spread = []
@@ -332,32 +348,92 @@
         tiled = jnp.concatenate([block] * (wide_cols // lanes), axis=1)
         spread.append(jnp.where(page == slot, tiled, 0.0))
     spread = jnp.concatenate(spread, axis=0).astype(jnp.bfloat16)
-    weights = up[...].reshape(wide_cols, features)
-    each = outs[0].shape[0]
     block = min(512, features)
     for start in range(0, features, block):
         made = jnp.dot(
-            spread, weights[:, start : start + block], preferred_element_type=jnp.float32
+            spread,
+            up[:, :, start : start + block].reshape(wide_cols, block),
+            preferred_element_type=jnp.float32,
         ).astype(jnp.bfloat16)
         for i, out in enumerate(outs):
             out[:, start : start + block] = made[i * each : (i + 1) * each]
 
 
-def small_call(kernel, where, adapters_of, slot_of, weights, arrays, outs, flops):
+def room(*shapes):
+    return pltpu.CompilerParams(
+        vmem_limit_bytes=(4 << 20) + sum(2 * math.prod(s) for s in shapes)
+    )
+
+
+def far(value):
+    return pltpu.with_memory_space_constraint(value, pltpu.HBM)
+
+
+def near(value):
+    return pltpu.with_memory_space_constraint(value, pltpu.VMEM)
+
+
+def small_call(kernel, scalars, weights, arrays, outs, flops):
     smem = pl.BlockSpec(memory_space=pltpu.SMEM)
-
-    def whole(x):
-        return pl.BlockSpec(x.shape, lambda i: (0,) * len(x.shape))
-
+    vmem = pl.BlockSpec(memory_space=pltpu.VMEM)
     moved = weights.size + sum(x.size for x in arrays)
+    arrays = [near(x) for x in arrays]
     return pl.pallas_call(
         kernel,
-        grid=(1,),
-        in_specs=[smem] * 3 + [whole(weights)] + [whole(x) for x in arrays],
-        out_specs=[whole(x) for x in outs],
-        out_shape=outs,
+        in_specs=[smem] * len(scalars) + [vmem] * (1 + len(arrays)),
+        out_specs=[vmem] * len(outs),
+        out_shape=[pltpu.VMEM(x.shape, x.dtype) for x in outs],
+        compiler_params=room(*[(4,) + x.shape for x in arrays + outs], (2,) + weights.shape),
         cost_estimate=pl.CostEstimate(flops=flops, bytes_accessed=2 * moved, transcendentals=0),
-    )(where, adapters_of, slot_of, weights, *arrays)
+    )(*scalars, near(weights), *arrays)
+
+
+def sum_kernel(*refs):
+    arrays, out = refs[:-1], refs[-1]
+    value = arrays[0][...].astype(jnp.float32)
+    for other in arrays[1:]:
+        value = value + other[...].astype(jnp.float32)
+    out[...] = value.astype(out.dtype)
+
+
+def add(a, b):
+    vmem = pl.BlockSpec(memory_space=pltpu.VMEM)
+    return pl.pallas_call(
+        sum_kernel,
+        in_specs=[vmem] * 2,
+        out_specs=vmem,
+        out_shape=pltpu.VMEM(a.shape, a.dtype),
+        compiler_params=room((4,) + a.shape),
+        cost_estimate=pl.CostEstimate(flops=a.size, bytes_accessed=6 * a.size, transcendentals=0),
+        name="add",
+    )(near(a), near(b))
+
+
+def finish_kernel(count, *refs):
+    wholes, parts, out = refs[:count], refs[count:-1], refs[-1]
+    each = parts[0].shape[0]
+    for i, part in enumerate(parts):
+        at = slice(i * each, (i + 1) * each)
+        value = part[...].astype(jnp.float32)
+        for other in wholes:
+            value = value + other[at, :].astype(jnp.float32)
+        out[at, :] = value.astype(out.dtype)
+
+
+def finish(wholes, parts):
+    vmem = pl.BlockSpec(memory_space=pltpu.VMEM)
+    shape = wholes[0].shape
+    return pl.pallas_call(
+        functools.partial(finish_kernel, len(wholes)),
+        in_specs=[vmem] * (len(wholes) + len(parts)),
+        out_specs=vmem,
+        out_shape=jax.ShapeDtypeStruct(shape, jnp.bfloat16),
+        compiler_params=room((4,) + shape),
+        cost_estimate=pl.CostEstimate(
+            flops=5 * math.prod(shape), bytes_accessed=12 * math.prod(shape), transcendentals=0
+        ),
+        name="finish",
+    )(*[near(x) for x in wholes], *[near(x) for x in parts])
 
 
 def after(value, *earlier):
@@ -380,9 +456,6 @@
     sections = lax.axis_size("section")
     pools = lax.axis_size("pool")
     splits = lax.axis_size("tp")
-    section = lax.axis_index("section")
-    pool = lax.axis_index("pool")
-    split = lax.axis_index("tp")
     groups = queries.shape[2]
     window_len = queries.shape[3]
     part = groups // CHUNKS
@@ -390,14 +463,18 @@
     pages_here, rank_width, features = adapter_down.shape
     own_width = adapter_up.shape[2]
     wide_cols = pages_here * rank_width
+    scalars = (
+        jnp.reshape(lax.axis_index("section"), (1,)).astype(jnp.int32),
+        jnp.reshape(lax.axis_index("pool"), (1,)).astype(jnp.int32),
+        request_adapter,
+        layer_page_slot,
+    )
 
     order = list(range(0, pools, 2)) + list(range(1, pools, 2))[::-1]
     ring = [(order[i], order[(i + 1) % pools]) for i in range(pools)]
     ring_next = [
         (s * pools + a, ((s + 1) % sections) * pools + b) for s in range(sections) for a, b in ring
     ]
-    forward = [(s, (s + 1) % sections) for s in range(sections)]
-    where = jnp.stack([section, pool]).astype(jnp.int32)
 
     def attend_part(c, asked):
         return attend(
@@ -413,32 +490,31 @@
     def gather(value):
         return lax.ppermute(value, "pool", ring)
 
-    offsets = list(range(splits - 1, 0, -1)) + [0]
-
-    def project_piece(i, *earlier):
-        d = offsets[i]
+    offsets = list(range(1, splits)) + [0]
+
+    def project_piece(i, earlier, added=()):
         first = after(contexts[0], *earlier)
-        piece = project([first] + contexts[1:], wo[0], split ^ d, splits)
+        return project([first] + contexts[1:], wo[0], offsets[i], splits, added)
+
+    def send_piece(i, piece):
         pairs = [
-            (s * splits + t, ((s + 1) % sections) * splits + (t ^ d))
+            (s * splits + t, ((s + 1) % sections) * splits + (t ^ offsets[i]))
             for s in range(sections)
             for t in range(splits)
         ]
-        arrived.append(lax.ppermute(piece, ("section", "tp"), pairs))
-        return piece
-
-    lanes = min(128, wide_cols)
+        return lax.ppermute(piece, ("section", "tp"), pairs)
+
+    lanes = min(2 * rank_width, wide_cols)
+    rank_rows = pools * part_rows // 2
 
     def rank_of(c, earlier):
         arrays = [after(held[c][0], earlier)] + held[c][1:]
         return small_call(
-            functools.partial(rank_kernel, order, list(range(pools)), c * part, part),
-            where,
-            request_adapter,
-            layer_page_slot,
+            functools.partial(rank_kernel, order, c * part, part),
+            scalars,
             adapter_down,
             arrays,
-            [jax.ShapeDtypeStruct((pools * part_rows, lanes), jnp.bfloat16)],
+            [jax.ShapeDtypeStruct((rank_rows, lanes), jnp.bfloat16)],
             2 * pools * part_rows * wide_cols * features,
         )[0]
 
@@ -447,68 +523,57 @@
         for d in range(splits - 1, 0, -1):
             pairs = [(t, t ^ d) for t in range(splits)]
             ranks.append(lax.ppermute(mine, "tp", pairs))
-        outs = small_call(
+        return small_call(
             functools.partial(up_kernel, order, c * part, part, len(ranks)),
-            where,
-            request_adapter,
-            layer_page_slot,
+            scalars,
             adapter_up,
             ranks,
             [jax.ShapeDtypeStruct((part_rows, own_width), jnp.bfloat16)] * pools,
             2 * pools * part_rows * wide_cols * own_width,
         )
-        return outs
 
     def scatter(step, value):
         if step == pools - 1:
             return lax.ppermute(value, ("section", "pool"), ring_next)
         return lax.ppermute(value, "pool", ring)
 
-    hidden_in = lax.ppermute(hidden[0, 0], "section", forward)
-    arrived = []
     contexts = [attend_part(0, queries[0, 0])]
     contexts.append(attend_part(1, after(queries[0, 0], contexts[0])))
     held = [[c] for c in contexts]
     held[0].append(gather(contexts[0]))
     held[0].append(gather(held[0][1]))
     held[1].append(gather(contexts[1]))
-    piece = project_piece(0, held[0][1])
-    held[0].append(gather(after(held[0][2], piece)))
-    piece = project_piece(1, piece, held[0][2])
-    held[1].append(gather(after(held[1][1], piece)))
-    piece = project_piece(2, piece, held[1][1])
+    pieces = [project_piece(0, [held[0][1]])]
+    arrived = [send_piece(0, pieces[0])]
+    held[0].append(gather(after(held[0][2], pieces[0])))
+    pieces.append(project_piece(1, [pieces[0], held[0][2]]))
+    arrived.append(send_piece(1, pieces[1]))
+    held[1].append(gather(after(held[1][1], pieces[1])))
+    pieces.append(project_piece(2, [pieces[1], held[1][1]]))
     for _ in range(4, pools):
         held[0].append(gather(held[0][-1]))
-    rank0 = rank_of(0, piece)
+    rank0 = rank_of(0, pieces[2])
     held[1].append(gather(after(held[1][2], rank0)))
     for _ in range(4, pools):
         held[1].append(gather(held[1][-1]))
     outs0 = up_of(0, rank0, held[1][2])
-    own0 = lax.ppermute(outs0[0], "section", forward)
     moving0 = scatter(1, outs0[1])
     rank1 = rank_of(1, outs0[0])
-    moving0 = scatter(2, after(moving0, rank1) + outs0[2])
+    moving0 = scatter(2, add(after(moving0, rank1), outs0[2]))
     outs1 = up_of(1, rank1, rank1)
-    own1 = lax.ppermute(outs1[0], "section", forward)
     moving1 = scatter(1, outs1[1])
-    piece = project_piece(3, piece, outs1[0])
-    moving0 = scatter(3, after(moving0, piece) + outs0[3])
-    moving1 = scatter(2, after(moving1, piece) + outs1[2])
-    moving1 = scatter(3, moving1 + outs1[3])
+    arrived.append(send_piece(2, after(pieces[2], outs1[0])))
+    moving0 = scatter(3, add(after(moving0, outs1[0]), outs0[3]))
+    added = add(after(moving1, outs1[0]), outs1[2])
+    moving1 = scatter(2, added)
+    pieces.append(project_piece(3, [pieces[2], added], [hidden[0, 0], outs0[0], outs1[0]]))
+    arrived.append(send_piece(3, pieces[3]))
+    moving1 = scatter(3, add(after(moving1, pieces[3]), outs1[3]))
     for step in range(4, pools):
-        moving0 = scatter(step, moving0 + outs0[step])
-        moving1 = scatter(step, moving1 + outs1[step])
-
-    base = hidden_in.astype(jnp.float32)
-    for piece in arrived:
-        base = base + piece.astype(jnp.float32)
-    delta = jnp.concatenate(
-        [
-            own0.astype(jnp.float32) + moving0.astype(jnp.float32),
-            own1.astype(jnp.float32) + moving1.astype(jnp.float32),
-        ]
-    )
-    return (base + delta).astype(jnp.bfloat16)[None, None]
+        moving0 = scatter(step, add(moving0, outs0[step]))
+        moving1 = scatter(step, add(moving1, outs1[step]))
+
+    return finish(arrived, [moving0, moving1])[None, None]
 
 
 def solution(mesh):

time: 128 us -> 101 us (0.79)
  waiting for transfers between devices: 43.1 us -> 29.1 us
  Pallas kernels: 48.9 us -> 37.5 us
  other arithmetic: 3.21 us -> 0 us
  starting transfers between devices: 29.5 us -> 32 us
    pallas_call x8 -> x13, Pallas kernels: 32.7 us -> 22.7 us  [the longest x4 15.7 us: project(): pl.pallas_call(functools.partial(project_kernel, len(chunks), len(added),...]
    ppermute x7 -> x4, waiting for transfers between devices: 17.2 us -> 8.33 us  [send_piece(): return lax.ppermute(piece, ('section', 'tp'), pairs)]
    ppermute x2, waiting for transfers between devices: 7.15 us -> 2.19 us  [scatter(): return lax.ppermute(value, ('section', 'pool'), ring_next)]
    ppermute x2, starting transfers between devices: 0.12 us -> 2.61 us  [scatter(): return lax.ppermute(value, ('section', 'pool'), ring_next)]
    ppermute x4, starting transfers between devices: 4.65 us -> 6.88 us  [scatter(): return lax.ppermute(value, 'pool', ring)]
    ppermute x7 -> x4, starting transfers between devices: 4.44 us -> 2.74 us  [send_piece(): return lax.ppermute(piece, ('section', 'tp'), pairs)]
    ppermute x6, waiting for transfers between devices: 5.93 us -> 7.49 us  [gather(): return lax.ppermute(value, 'pool', ring)]
    pallas_call x2, Pallas kernels: 16.2 us -> 14.8 us  [attend(): pl.pallas_call(functools.partial(attend_kernel, first), grid=(1,), in_spe...]
  transfers between devices with their start and end apart: 25 -> 22, of which waited for: 15 -> 13; matrix products, arithmetic and copies ran while one was open for 2% -> 0% of each run, Pallas kernels for 30% -> 29%
where the time goes in v2:
time: 101 us; the launch traced here: 100 us
  Pallas kernels  37.5 us (37%)
  starting transfers between devices  32 us (32%)
  waiting for transfers between devices  29.1 us (29%)
  local copies, waits for them, and re-layouts  1.47 us (1%)
    pallas_call x4, Pallas kernels, project(): pl.pallas_call(functools.partial(project_kernel, len(chunks), len(added),...  15.7 us
    pallas_call x2, Pallas kernels, attend(): pl.pallas_call(functools.partial(attend_kernel, first), grid=(1,), in_spe...  14.8 us
    ppermute x6, starting transfers between devices, gather(): return lax.ppermute(value, 'pool', ring)  12.7 us
    ppermute x4, waiting for transfers between devices, send_piece(): return lax.ppermute(piece, ('section', 'tp'), pairs)  8.33 us
    ppermute x6, waiting for transfers between devices, gather(): return lax.ppermute(value, 'pool', ring)  7.49 us
    ppermute x6, starting transfers between devices, up_of(): ranks.append(lax.ppermute(mine, 'tp', pairs))  7.04 us
    ppermute x4, starting transfers between devices, scatter(): return lax.ppermute(value, 'pool', ring)  6.88 us
    ppermute x6, waiting for transfers between devices, up_of(): ranks.append(lax.ppermute(mine, 'tp', pairs))  6.7 us
  transfers between devices with their start and end apart: 22, of which 13 were waited for; matrix products, arithmetic and copies ran while one was open for 0% of the time, Pallas kernels for 29%

profile of v2, /device:TPU:0, one launch (start us, length us, event | category | flops | bytes accessed | tf_op | source)
XLA Modules:
  0.0 100.3 jit_solution(9494438695940750979)
XLA Ops:
  0.0 0.7 copy-done.4
  0.7 0.7 copy-done.6
  1.4 7.4 %attend.2.refs_0_ = bf16[64,2048]{1,0:T(8,128)(2,1)S(1)} custom-call(s32[16]{0:T(128)S(1)} %bitcast.15, s32[16,16]{1,0:T(8,128)S(1)} %bitcast.13, bf16[16,128,128]{2,1,0:T(8,128)(2,1)} %bitcast.23, bf16[16,2,2,8,128]{4,3,2,1,0:T(8,128)(2,1)} %bitcast.25, bf16[128,2,2,64,128]{4,3,2,1,0:T(8,128)(2,1)} %bitcast.21), custom_call_target="tpu_custom_call" | custom-call | flops 500000000 | bytes 12000000 | tf_op jit(solution)/shard_map/attend/pallas_call | solution.py:180
  8.7 4.9 %collective-permute-start = (bf16[64,2048]{1,0:T(8,128)(2,1)S(1)}, bf16[64,2048]{1,0:T(8,128)(2,1)S(1)}, u32[]{:S(2)}, u32[]{:S(2)}) collective-permute-start(bf16[64,2048]{1,0:T(8,128)(2,1)S(1)} %attend.2.refs_0_), channel_id=1, source_target_pairs={{0,2},{2,3},{3,1},{1,0},{4,6},{6,7},{7,5},{5,4},{8,10},{10,11},{11... | collective-permute-start | bytes 786440 | tf_op jit(solution)/shard_map/ppermute | solution.py:491
  13.6 5.6 %collective-permute-done.refs_1_ = bf16[64,2048]{1,0:T(8,128)(2,1)S(1)} collective-permute-done((bf16[64,2048]{1,0:T(8,128)(2,1)S(1)}, bf16[64,2048]{1,0:T(8,128)(2,1)S(1)}, u32[]{:S(2)}, u32[]{:S(2)}) %collective-permute-start) | collective-permute-done | bytes 262176 | tf_op jit(solution)/shard_map/ppermute | solution.py:491
  19.2 3.4 %collective-permute-start.2 = (bf16[64,2048]{1,0:T(8,128)(2,1)S(1)}, bf16[64,2048]{1,0:T(8,128)(2,1)S(1)}, u32[]{:S(2)}, u32[]{:S(2)}) collective-permute-start(bf16[64,2048]{1,0:T(8,128)(2,1)S(1)} %collective-permute-done.refs_1_), channel_id=1, source_target_pairs={{0,2},{2,3},{3,1},{1,0},{4,6},{6,7},{7,5},{5,4},{8,10},{10,11},{11... | collective-permute-start | bytes 786440 | tf_op jit(solution)/shard_map/ppermute | solution.py:491
  22.6 7.5 %attend.3.refs_1_.refs_0_ = bf16[64,2048]{1,0:T(8,128)(2,1)S(1)} custom-call(s32[16]{0:T(128)S(1)} %bitcast.16, s32[16,16]{1,0:T(8,128)S(1)} %bitcast.14, bf16[16,128,128]{2,1,0:T(8,128)(2,1)} %bitcast.24, bf16[16,2,2,8,128]{4,3,2,1,0:T(8,128)(2,1)} %bitcast.26, bf16[128,2,2,64,128]{4,3,2,1,0:T(8,128)(2,1)} %bitcast.22), custom_call_target="tpu_custom_call" | custom-call | flops 500000000 | bytes 12000000 | tf_op jit(solution)/shard_map/attend/pallas_call | solution.py:180
  30.1 0.8 collective-permute-start.4
  30.8 3.9 %project.4 = bf16[128,2048]{1,0:T(8,128)(2,1)S(1)} custom-call(bf16[64,2048]{1,0:T(8,128)(2,1)S(1)} %attend.2.refs_0_, bf16[64,2048]{1,0:T(8,128)(2,1)S(1)} %attend.3.refs_1_.refs_0_, bf16[2048,8192]{1,0:T(8,128)(2,1)} %bitcast.17), custom_call_target="tpu_custom_call" | custom-call | flops 1073741824 | bytes 9437184 | tf_op jit(solution)/shard_map/project/pallas_call | solution.py:251
  34.7 0.0 collective-permute-done.2.refs_2_
  34.8 1.2 %collective-permute-start.5 = (bf16[64,2048]{1,0:T(8,128)(2,1)S(1)}, bf16[64,2048]{1,0:T(8,128)(2,1)S(1)}, u32[]{:S(2)}, u32[]{:S(2)}) collective-permute-start(bf16[64,2048]{1,0:T(8,128)(2,1)S(1)} %collective-permute-done.2.refs_2_), channel_id=1, source_target_pairs={{0,2},{2,3},{3,1},{1,0},{4,6},{6,7},{7,5},{5,4},{8,10},{10,11},{11... | collective-permute-start | bytes 786440 | tf_op jit(solution)/shard_map/ppermute | solution.py:491
  35.9 3.9 %project.5 = bf16[128,2048]{1,0:T(8,128)(2,1)S(1)} custom-call(bf16[64,2048]{1,0:T(8,128)(2,1)S(1)} %attend.2.refs_0_, bf16[64,2048]{1,0:T(8,128)(2,1)S(1)} %attend.3.refs_1_.refs_0_, bf16[2048,8192]{1,0:T(8,128)(2,1)} %bitcast.18), custom_call_target="tpu_custom_call" | custom-call | flops 1073741824 | bytes 9437184 | tf_op jit(solution)/shard_map/project/pallas_call | solution.py:251
  39.9 0.0 collective-permute-done.4.refs_1_
  39.9 0.9 collective-permute-start.6
  40.7 4.1 %project.6 = bf16[128,2048]{1,0:T(8,128)(2,1)S(1)} custom-call(bf16[64,2048]{1,0:T(8,128)(2,1)S(1)} %attend.2.refs_0_, bf16[64,2048]{1,0:T(8,128)(2,1)S(1)} %attend.3.refs_1_.refs_0_, bf16[2048,8192]{1,0:T(8,128)(2,1)} %bitcast.19), custom_call_target="tpu_custom_call" | custom-call | flops 1073741824 | bytes 9437184 | tf_op jit(solution)/shard_map/project/pallas_call | solution.py:251
  44.8 0.0 copy-start.2
  44.8 0.0 collective-permute-done.5.refs_3_
  44.8 0.1 copy-done
  44.9 0.0 copy-done.3
  44.9 1.4 %shard_map.109.refs_0_ = bf16[128,128]{1,0:T(8,128)(2,1)S(1)} custom-call(s32[1]{0:T(128)} %bitcast.8.section, s32[1]{0:T(128)} %bitcast.9.pool, s32[2,4,16]{2,1,0:T(4,128)S(1)} %copy-done.3, s32[64]{0:T(128)S(1)} %copy-done.5, bf16[8,64,2048]{2,1,0:T(8,128)(2,1)S(1)} %copy-done, bf16[64,2048]{1,0:T(8,128)(2,1)S(1)} %attend.2.refs_0_, ...), custom_call_target="tpu_custom_call" | custom-call | flops 536870912 | bytes 3145728 | tf_op jit(solution)/shard_map/pallas_call | solution.py:381
  46.4 1.9 %collective-permute-done.6.refs_2_ = bf16[64,2048]{1,0:T(8,128)(2,1)S(1)} collective-permute-done((bf16[64,2048]{1,0:T(8,128)(2,1)S(1)}, bf16[64,2048]{1,0:T(8,128)(2,1)S(1)}, u32[]{:S(2)}, u32[]{:S(2)}) %collective-permute-start.6) | collective-permute-done | bytes 262176 | tf_op jit(solution)/shard_map/ppermute | solution.py:491
  48.2 1.6 %collective-permute-start.10 = (bf16[64,2048]{1,0:T(8,128)(2,1)S(1)}, bf16[64,2048]{1,0:T(8,128)(2,1)S(1)}, u32[]{:S(2)}, u32[]{:S(2)}) collective-permute-start(bf16[64,2048]{1,0:T(8,128)(2,1)S(1)} %collective-permute-done.6.refs_2_), channel_id=1, source_target_pairs={{0,2},{2,3},{3,1},{1,0},{4,6},{6,7},{7,5},{5,4},{8,10},{10,11},{11... | collective-permute-start | bytes 786440 | tf_op jit(solution)/shard_map/ppermute | solution.py:491
  49.9 1.5 %collective-permute-start.9 = (bf16[128,128]{1,0:T(8,128)(2,1)S(1)}, bf16[128,128]{1,0:T(8,128)(2,1)S(1)}, u32[]{:S(2)}, u32[]{:S(2)}) collective-permute-start(bf16[128,128]{1,0:T(8,128)(2,1)S(1)} %shard_map.109.refs_0_), channel_id=1, source_target_pairs={{0,4},{4,0},{8,12},{12,8},{1,5},{5,1},{9,13},{13,9},{2,6},{6,2},{1... | collective-permute-start | bytes 98312 | tf_op jit(solution)/shard_map/ppermute | solution.py:525
  51.4 1.5 %collective-permute-start.8 = (bf16[128,128]{1,0:T(8,128)(2,1)S(1)}, bf16[128,128]{1,0:T(8,128)(2,1)S(1)}, u32[]{:S(2)}, u32[]{:S(2)}) collective-permute-start(bf16[128,128]{1,0:T(8,128)(2,1)S(1)} %shard_map.109.refs_0_), channel_id=1, source_target_pairs={{0,8},{4,12},{8,0},{12,4},{1,9},{5,13},{9,1},{13,5},{2,10},{6,14},... | collective-permute-start | bytes 98312 | tf_op jit(solution)/shard_map/ppermute | solution.py:525
  52.9 0.5 collective-permute-start.7
  53.4 0.8 collective-permute-done.9.refs_3_
  54.1 1.2 %collective-permute-done.8.refs_2_ = bf16[128,128]{1,0:T(8,128)(2,1)S(1)} collective-permute-done((bf16[128,128]{1,0:T(8,128)(2,1)S(1)}, bf16[128,128]{1,0:T(8,128)(2,1)S(1)}, u32[]{:S(2)}, u32[]{:S(2)}) %collective-permute-start.8) | collective-permute-done | bytes 32800 | tf_op jit(solution)/shard_map/ppermute | solution.py:525
  55.4 2.3 %collective-permute-done.7.refs_1_ = bf16[128,128]{1,0:T(8,128)(2,1)S(1)} collective-permute-done((bf16[128,128]{1,0:T(8,128)(2,1)S(1)}, bf16[128,128]{1,0:T(8,128)(2,1)S(1)}, u32[]{:S(2)}, u32[]{:S(2)}) %collective-permute-start.7) | collective-permute-done | bytes 32800 | tf_op jit(solution)/shard_map/ppermute | solution.py:525
  57.7 1.4 %shard_map.110 = (bf16[64,2048]{1,0:T(8,128)(2,1)S(1)}, bf16[64,2048]{1,0:T(8,128)(2,1)S(1)}, bf16[64,2048]{1,0:T(8,128)(2,1)S(1)}, bf16[64,2048]{1,0:T(8,128)(2,1)S(1)}) custom-call(s32[1]{0:T(128)} %bitcast.8.section, s32[1]{0:T(128)} %bitcast.9.pool, s32[2,4,16]{2,1,0:T(4,128)S(1)} %copy-done.3, s32[64]{0:T(128)S(1)} %copy-done.5, ...), custom_call_target="tpu_custom_call" | custom-call | flops 536870912 | bytes 2228224 | tf_op jit(solution)/shard_map/pallas_call | solution.py:381
  59.1 0.5 collective-permute-start.17
  59.6 0.0 collective-permute-done.10.refs_3_
  59.6 1.4 %shard_map.111.refs_0_ = bf16[128,128]{1,0:T(8,128)(2,1)S(1)} custom-call(s32[1]{0:T(128)} %bitcast.8.section, s32[1]{0:T(128)} %bitcast.9.pool, s32[2,4,16]{2,1,0:T(4,128)S(1)} %copy-done.3, s32[64]{0:T(128)S(1)} %copy-done.5, bf16[8,64,2048]{2,1,0:T(8,128)(2,1)S(1)} %copy-done, bf16[64,2048]{1,0:T(8,128)(2,1)S(1)} %attend.3.refs_1_.refs_0_, ...), custom_call_target="tpu_custom_call" | custom-call | flops 536870912 | bytes 3145728 | tf_op jit(solution)/shard_map/pallas_call | solution.py:381
  61.0 0.6 collective-permute-start.13
  61.6 0.5 collective-permute-start.12
  62.1 2.5 %collective-permute-start.11 = (bf16[128,128]{1,0:T(8,128)(2,1)S(1)}, bf16[128,128]{1,0:T(8,128)(2,1)S(1)}, u32[]{:S(2)}, u32[]{:S(2)}) collective-permute-start(bf16[128,128]{1,0:T(8,128)(2,1)S(1)} %shard_map.111.refs_0_), channel_id=1, source_target_pairs={{0,12},{4,8},{8,4},{12,0},{1,13},{5,9},{9,5},{13,1},{2,14},{6,10},... | collective-permute-start | bytes 98312 | tf_op jit(solution)/shard_map/ppermute | solution.py:525
  64.6 0.4 collective-permute-done.13.refs_3_
  65.0 0.5 collective-permute-done.12.refs_2_
  65.5 1.4 %collective-permute-done.11.refs_1_ = bf16[128,128]{1,0:T(8,128)(2,1)S(1)} collective-permute-done((bf16[128,128]{1,0:T(8,128)(2,1)S(1)}, bf16[128,128]{1,0:T(8,128)(2,1)S(1)}, u32[]{:S(2)}, u32[]{:S(2)}) %collective-permute-start.11) | collective-permute-done | bytes 32800 | tf_op jit(solution)/shard_map/ppermute | solution.py:525
  66.9 1.4 %shard_map.112 = (bf16[64,2048]{1,0:T(8,128)(2,1)S(1)}, bf16[64,2048]{1,0:T(8,128)(2,1)S(1)}, bf16[64,2048]{1,0:T(8,128)(2,1)S(1)}, bf16[64,2048]{1,0:T(8,128)(2,1)S(1)}) custom-call(s32[1]{0:T(128)} %bitcast.8.section, s32[1]{0:T(128)} %bitcast.9.pool, s32[2,4,16]{2,1,0:T(4,128)S(1)} %copy-done.3, s32[64]{0:T(128)S(1)} %copy-done.5, ...), custom_call_target="tpu_custom_call" | custom-call | flops 536870912 | bytes 2228224 | tf_op jit(solution)/shard_map/pallas_call | solution.py:381
  68.3 2.2 %collective-permute-start.15 = (bf16[64,2048]{1,0:T(8,128)(2,1)S(1)}, bf16[64,2048]{1,0:T(8,128)(2,1)S(1)}, u32[]{:S(2)}, u32[]{:S(2)}) collective-permute-start(bf16[64,2048]{1,0:T(8,128)(2,1)S(1)} %get-tuple-element.44), channel_id=1, source_target_pairs={{0,2},{2,3},{3,1},{1,0},{4,6},{6,7},{7,5},{5,4},{8,10},{10,11},{11... | collective-permute-start | bytes 786440 | tf_op jit(solution)/shard_map/ppermute | solution.py:538
  70.5 0.0 collective-permute-start.1
  70.5 0.0 collective-permute-done.17.refs_0_
  70.5 0.1 add.5
  70.6 0.8 collective-permute-start.18
  71.3 2.4 %collective-permute-start.3 = (bf16[128,2048]{1,0:T(8,128)(2,1)S(1)}, bf16[128,2048]{1,0:T(8,128)(2,1)S(1)}, u32[]{:S(2)}, u32[]{:S(2)}) collective-permute-start(bf16[128,2048]{1,0:T(8,128)(2,1)S(1)} %project.5), channel_id=1, source_target_pairs={{0,24},{4,28},{8,16},{12,20},{16,8},{20,12},{24,0},{28,4},{1,25},{... | collective-permute-start | bytes 1572872 | tf_op jit(solution)/shard_map/ppermute | solution.py:505
  73.8 0.2 collective-permute-start.14
  74.0 1.7 %collective-permute-done.15.refs_0_ = bf16[64,2048]{1,0:T(8,128)(2,1)S(1)} collective-permute-done((bf16[64,2048]{1,0:T(8,128)(2,1)S(1)}, bf16[64,2048]{1,0:T(8,128)(2,1)S(1)}, u32[]{:S(2)}, u32[]{:S(2)}) %collective-permute-start.15) | collective-permute-done | bytes 262176 | tf_op jit(solution)/shard_map/ppermute | solution.py:538
  75.7 0.1 add.4
  75.8 3.4 %collective-permute-start.20 = (bf16[64,2048]{1,0:T(8,128)(2,1)S(1)}, bf16[64,2048]{1,0:T(8,128)(2,1)S(1)}, u32[]{:S(2)}, u32[]{:S(2)}) collective-permute-start(bf16[64,2048]{1,0:T(8,128)(2,1)S(1)} %add.4), channel_id=1, source_target_pairs={{0,2},{2,3},{3,1},{1,0},{4,6},{6,7},{7,5},{5,4},{8,10},{10,11},{11... | collective-permute-start | bytes 786440 | tf_op jit(solution)/shard_map/ppermute | solution.py:538
  79.2 3.9 %project.7 = bf16[128,2048]{1,0:T(8,128)(2,1)S(1)} custom-call(bf16[64,2048]{1,0:T(8,128)(2,1)S(1)} %attend.2.refs_0_, bf16[64,2048]{1,0:T(8,128)(2,1)S(1)} %attend.3.refs_1_.refs_0_, bf16[2048,8192]{1,0:T(8,128)(2,1)} %bitcast.20, bf16[128,2048]{1,0:T(8,128)(2,1)S(1)} %bitcast.12, bf16[64,2048]{1,0:T(8,128)(2,1)S(1)} %get-tuple-element.38.refs_4_, ...), custom_call_target="tpu_custom_call" | custom-call | flops 1073741824 | bytes 9437184 | tf_op jit(solution)/shard_map/project/pallas_call | solution.py:251
  83.1 0.0 collective-permute-done.18.refs_0_
  83.1 0.1 collective-permute-start.16
  83.2 0.1 add.6
  83.3 2.7 %collective-permute-done.20.refs_0_ = bf16[64,2048]{1,0:T(8,128)(2,1)S(1)} collective-permute-done((bf16[64,2048]{1,0:T(8,128)(2,1)S(1)}, bf16[64,2048]{1,0:T(8,128)(2,1)S(1)}, u32[]{:S(2)}, u32[]{:S(2)}) %collective-permute-start.20) | collective-permute-done | bytes 262176 | tf_op jit(solution)/shard_map/ppermute | solution.py:538
  86.0 1.4 %collective-permute-start.19 = (bf16[64,2048]{1,0:T(8,128)(2,1)S(1)}, bf16[64,2048]{1,0:T(8,128)(2,1)S(1)}, u32[]{:S(2)}, u32[]{:S(2)}) collective-permute-start(bf16[64,2048]{1,0:T(8,128)(2,1)S(1)} %add.6), channel_id=1, source_target_pairs={{0,18},{2,19},{3,17},{1,16},{16,2},{18,3},{19,1},{17,0},{4,22},{6,... | collective-permute-start | bytes 786440 | tf_op jit(solution)/shard_map/ppermute | solution.py:537
  87.4 0.1 add.7
  87.4 0.0 collective-permute-done.1.refs_0_
  87.4 1.2 %collective-permute-start.21 = (bf16[64,2048]{1,0:T(8,128)(2,1)S(1)}, bf16[64,2048]{1,0:T(8,128)(2,1)S(1)}, u32[]{:S(2)}, u32[]{:S(2)}) collective-permute-start(bf16[64,2048]{1,0:T(8,128)(2,1)S(1)} %add.7), channel_id=1, source_target_pairs={{0,18},{2,19},{3,17},{1,16},{16,2},{18,3},{19,1},{17,0},{4,22},{6,... | collective-permute-start | bytes 786440 | tf_op jit(solution)/shard_map/ppermute | solution.py:537
  88.6 7.2 %collective-permute-done.3.refs_1_ = bf16[128,2048]{1,0:T(8,128)(2,1)S(1)} collective-permute-done((bf16[128,2048]{1,0:T(8,128)(2,1)S(1)}, bf16[128,2048]{1,0:T(8,128)(2,1)S(1)}, u32[]{:S(2)}, u32[]{:S(2)}) %collective-permute-start.3) | collective-permute-done | bytes 524320 | tf_op jit(solution)/shard_map/ppermute | solution.py:505
  95.8 1.2 %collective-permute-done.14.refs_2_ = bf16[128,2048]{1,0:T(8,128)(2,1)S(1)} collective-permute-done((bf16[128,2048]{1,0:T(8,128)(2,1)S(1)}, bf16[128,2048]{1,0:T(8,128)(2,1)S(1)}, u32[]{:S(2)}, u32[]{:S(2)}) %collective-permute-start.14) | collective-permute-done | bytes 524320 | tf_op jit(solution)/shard_map/ppermute | solution.py:505
  97.0 0.0 collective-permute-done.19.refs_4_
  97.0 2.2 %collective-permute-done.21.refs_5_ = bf16[64,2048]{1,0:T(8,128)(2,1)S(1)} collective-permute-done((bf16[64,2048]{1,0:T(8,128)(2,1)S(1)}, bf16[64,2048]{1,0:T(8,128)(2,1)S(1)}, u32[]{:S(2)}, u32[]{:S(2)}) %collective-permute-start.21) | collective-permute-done | bytes 262176 | tf_op jit(solution)/shard_map/ppermute | solution.py:537
  99.2 0.0 collective-permute-done.16.refs_3_
  99.2 1.1 %finish.1 = bf16[128,2048]{1,0:T(8,128)(2,1)} custom-call(bf16[128,2048]{1,0:T(8,128)(2,1)S(1)} %collective-permute-done.1.refs_0_, bf16[128,2048]{1,0:T(8,128)(2,1)S(1)} %collective-permute-done.3.refs_1_, bf16[128,2048]{1,0:T(8,128)(2,1)S(1)} %collective-permute-done.14.refs_2_, bf16[128,2048]{1,0:T(8,128)(2,1)S(1)} %collective-permute-done.16.refs_3_, ...), custom_call_target="tpu_custom_call" | custom-call | flops 1310720 | bytes 3145728 | tf_op jit(solution)/shard_map/finish/pallas_call | solution.py:426
  (9 shorter events, 0.0 us)
Async XLA Ops:
  0.0 0.7 copy-start.4
  0.7 0.7 copy-start.6
  8.7 10.5 %collective-permute-start = (bf16[64,2048]{1,0:T(8,128)(2,1)S(1)}, bf16[64,2048]{1,0:T(8,128)(2,1)S(1)}, u32[]{:S(2)}, u32[]{:S(2)}) collective-permute-start(bf16[64,2048]{1,0:T(8,128)(2,1)S(1)} %attend.2.refs_0_), channel_id=1, source_target_pairs={{0,2},{2,3},{3,1},{1,0},{4,6},{6,7},{7,5},{5,4},{8,10},{10,11},{11... | collective-permute-start | bytes 786440 | tf_op jit(solution)/shard_map/ppermute | solution.py:491
  19.2 15.5 %collective-permute-start.2 = (bf16[64,2048]{1,0:T(8,128)(2,1)S(1)}, bf16[64,2048]{1,0:T(8,128)(2,1)S(1)}, u32[]{:S(2)}, u32[]{:S(2)}) collective-permute-start(bf16[64,2048]{1,0:T(8,128)(2,1)S(1)} %collective-permute-done.refs_1_), channel_id=1, source_target_pairs={{0,2},{2,3},{3,1},{1,0},{4,6},{6,7},{7,5},{5,4},{8,10},{10,11},{11... | collective-permute-start | bytes 786440 | tf_op jit(solution)/shard_map/ppermute | solution.py:491
  30.1 9.8 %collective-permute-start.4 = (bf16[64,2048]{1,0:T(8,128)(2,1)S(1)}, bf16[64,2048]{1,0:T(8,128)(2,1)S(1)}, u32[]{:S(2)}, u32[]{:S(2)}) collective-permute-start(bf16[64,2048]{1,0:T(8,128)(2,1)S(1)} %attend.3.refs_1_.refs_0_), channel_id=1, source_target_pairs={{0,2},{2,3},{3,1},{1,0},{4,6},{6,7},{7,5},{5,4},{8,10},{10,11},{11... | collective-permute-start | bytes 786440 | tf_op jit(solution)/shard_map/ppermute | solution.py:491
  34.8 10.1 %collective-permute-start.5 = (bf16[64,2048]{1,0:T(8,128)(2,1)S(1)}, bf16[64,2048]{1,0:T(8,128)(2,1)S(1)}, u32[]{:S(2)}, u32[]{:S(2)}) collective-permute-start(bf16[64,2048]{1,0:T(8,128)(2,1)S(1)} %collective-permute-done.2.refs_2_), channel_id=1, source_target_pairs={{0,2},{2,3},{3,1},{1,0},{4,6},{6,7},{7,5},{5,4},{8,10},{10,11},{11... | collective-permute-start | bytes 786440 | tf_op jit(solution)/shard_map/ppermute | solution.py:491
  39.9 8.4 %collective-permute-start.6 = (bf16[64,2048]{1,0:T(8,128)(2,1)S(1)}, bf16[64,2048]{1,0:T(8,128)(2,1)S(1)}, u32[]{:S(2)}, u32[]{:S(2)}) collective-permute-start(bf16[64,2048]{1,0:T(8,128)(2,1)S(1)} %collective-permute-done.4.refs_1_), channel_id=1, source_target_pairs={{0,2},{2,3},{3,1},{1,0},{4,6},{6,7},{7,5},{5,4},{8,10},{10,11},{11... | collective-permute-start | bytes 786440 | tf_op jit(solution)/shard_map/ppermute | solution.py:491
  40.7 4.2 %copy-start = (bf16[8,64,2048]{2,1,0:T(8,128)(2,1)S(1)}, bf16[8,64,2048]{2,1,0:T(8,128)(2,1)}, u32[]{:S(2)}) copy-start(bf16[8,64,2048]{2,1,0:T(8,128)(2,1)} %down.3) | copy-start | bytes 6291460
  40.7 4.2 %copy-start.3 = (s32[2,4,16]{2,1,0:T(4,128)S(1)}, s32[2,4,16]{2,1,0:T(4,128)}, u32[]{:S(2)}) copy-start(s32[2,4,16]{2,1,0:T(4,128)} %adapters_of.7) | copy-start | bytes 1540
  40.7 4.2 %copy-start.5 = (s32[64]{0:T(128)S(1)}, s32[64]{0:T(128)}, u32[]{:S(2)}) copy-start(s32[64]{0:T(128)} %slot_of.7) | copy-start | bytes 772
  40.7 17.0 %copy-start.1 = (bf16[8,64,2048]{2,1,0:T(8,128)(2,1)S(1)}, bf16[8,64,2048]{2,1,0:T(8,128)(2,1)}, u32[]{:S(2)}) copy-start(bf16[8,64,2048]{2,1,0:T(8,128)(2,1)} %up.3) | copy-start | bytes 6291460
  44.8 34.4 %copy-start.2 = (bf16[1,1,128,2048]{3,2,1,0:T(8,128)(2,1)S(1)}, bf16[1,1,128,2048]{3,2,1,0:T(8,128)(2,1)}, u32[]{:S(2)}) copy-start(bf16[1,1,128,2048]{3,2,1,0:T(8,128)(2,1)} %param.11) | copy-start | bytes 1572868
  48.2 11.4 %collective-permute-start.10 = (bf16[64,2048]{1,0:T(8,128)(2,1)S(1)}, bf16[64,2048]{1,0:T(8,128)(2,1)S(1)}, u32[]{:S(2)}, u32[]{:S(2)}) collective-permute-start(bf16[64,2048]{1,0:T(8,128)(2,1)S(1)} %collective-permute-done.6.refs_2_), channel_id=1, source_target_pairs={{0,2},{2,3},{3,1},{1,0},{4,6},{6,7},{7,5},{5,4},{8,10},{10,11},{11... | collective-permute-start | bytes 786440 | tf_op jit(solution)/shard_map/ppermute | solution.py:491
  49.9 4.3 %collective-permute-start.9 = (bf16[128,128]{1,0:T(8,128)(2,1)S(1)}, bf16[128,128]{1,0:T(8,128)(2,1)S(1)}, u32[]{:S(2)}, u32[]{:S(2)}) collective-permute-start(bf16[128,128]{1,0:T(8,128)(2,1)S(1)} %shard_map.109.refs_0_), channel_id=1, source_target_pairs={{0,4},{4,0},{8,12},{12,8},{1,5},{5,1},{9,13},{13,9},{2,6},{6,2},{1... | collective-permute-start | bytes 98312 | tf_op jit(solution)/shard_map/ppermute | solution.py:525
  51.4 4.0 %collective-permute-start.8 = (bf16[128,128]{1,0:T(8,128)(2,1)S(1)}, bf16[128,128]{1,0:T(8,128)(2,1)S(1)}, u32[]{:S(2)}, u32[]{:S(2)}) collective-permute-start(bf16[128,128]{1,0:T(8,128)(2,1)S(1)} %shard_map.109.refs_0_), channel_id=1, source_target_pairs={{0,8},{4,12},{8,0},{12,4},{1,9},{5,13},{9,1},{13,5},{2,10},{6,14},... | collective-permute-start | bytes 98312 | tf_op jit(solution)/shard_map/ppermute | solution.py:525
  52.9 4.8 %collective-permute-start.7 = (bf16[128,128]{1,0:T(8,128)(2,1)S(1)}, bf16[128,128]{1,0:T(8,128)(2,1)S(1)}, u32[]{:S(2)}, u32[]{:S(2)}) collective-permute-start(bf16[128,128]{1,0:T(8,128)(2,1)S(1)} %shard_map.109.refs_0_), channel_id=1, source_target_pairs={{0,12},{4,8},{8,4},{12,0},{1,13},{5,9},{9,5},{13,1},{2,14},{6,10},... | collective-permute-start | bytes 98312 | tf_op jit(solution)/shard_map/ppermute | solution.py:525
  59.1 11.4 %collective-permute-start.17 = (bf16[64,2048]{1,0:T(8,128)(2,1)S(1)}, bf16[64,2048]{1,0:T(8,128)(2,1)S(1)}, u32[]{:S(2)}, u32[]{:S(2)}) collective-permute-start(bf16[64,2048]{1,0:T(8,128)(2,1)S(1)} %get-tuple-element.48), channel_id=1, source_target_pairs={{0,2},{2,3},{3,1},{1,0},{4,6},{6,7},{7,5},{5,4},{8,10},{10,11},{11... | collective-permute-start | bytes 786440 | tf_op jit(solution)/shard_map/ppermute | solution.py:538
  61.0 4.0 %collective-permute-start.13 = (bf16[128,128]{1,0:T(8,128)(2,1)S(1)}, bf16[128,128]{1,0:T(8,128)(2,1)S(1)}, u32[]{:S(2)}, u32[]{:S(2)}) collective-permute-start(bf16[128,128]{1,0:T(8,128)(2,1)S(1)} %shard_map.111.refs_0_), channel_id=1, source_target_pairs={{0,4},{4,0},{8,12},{12,8},{1,5},{5,1},{9,13},{13,9},{2,6},{6,2},{1... | collective-permute-start | bytes 98312 | tf_op jit(solution)/shard_map/ppermute | solution.py:525
  61.6 3.9 %collective-permute-start.12 = (bf16[128,128]{1,0:T(8,128)(2,1)S(1)}, bf16[128,128]{1,0:T(8,128)(2,1)S(1)}, u32[]{:S(2)}, u32[]{:S(2)}) collective-permute-start(bf16[128,128]{1,0:T(8,128)(2,1)S(1)} %shard_map.111.refs_0_), channel_id=1, source_target_pairs={{0,8},{4,12},{8,0},{12,4},{1,9},{5,13},{9,1},{13,5},{2,10},{6,14},... | collective-permute-start | bytes 98312 | tf_op jit(solution)/shard_map/ppermute | solution.py:525
  62.1 4.8 %collective-permute-start.11 = (bf16[128,128]{1,0:T(8,128)(2,1)S(1)}, bf16[128,128]{1,0:T(8,128)(2,1)S(1)}, u32[]{:S(2)}, u32[]{:S(2)}) collective-permute-start(bf16[128,128]{1,0:T(8,128)(2,1)S(1)} %shard_map.111.refs_0_), channel_id=1, source_target_pairs={{0,12},{4,8},{8,4},{12,0},{1,13},{5,9},{9,5},{13,1},{2,14},{6,10},... | collective-permute-start | bytes 98312 | tf_op jit(solution)/shard_map/ppermute | solution.py:525
  68.3 7.4 %collective-permute-start.15 = (bf16[64,2048]{1,0:T(8,128)(2,1)S(1)}, bf16[64,2048]{1,0:T(8,128)(2,1)S(1)}, u32[]{:S(2)}, u32[]{:S(2)}) collective-permute-start(bf16[64,2048]{1,0:T(8,128)(2,1)S(1)} %get-tuple-element.44), channel_id=1, source_target_pairs={{0,2},{2,3},{3,1},{1,0},{4,6},{6,7},{7,5},{5,4},{8,10},{10,11},{11... | collective-permute-start | bytes 786440 | tf_op jit(solution)/shard_map/ppermute | solution.py:538
  70.5 16.9 %collective-permute-start.1 = (bf16[128,2048]{1,0:T(8,128)(2,1)S(1)}, bf16[128,2048]{1,0:T(8,128)(2,1)S(1)}, u32[]{:S(2)}, u32[]{:S(2)}) collective-permute-start(bf16[128,2048]{1,0:T(8,128)(2,1)S(1)} %project.4), channel_id=1, source_target_pairs={{0,20},{4,16},{8,28},{12,24},{16,4},{20,0},{24,12},{28,8},{1,21},{... | collective-permute-start | bytes 1572872 | tf_op jit(solution)/shard_map/ppermute | solution.py:505
  70.6 12.6 %collective-permute-start.18 = (bf16[64,2048]{1,0:T(8,128)(2,1)S(1)}, bf16[64,2048]{1,0:T(8,128)(2,1)S(1)}, u32[]{:S(2)}, u32[]{:S(2)}) collective-permute-start(bf16[64,2048]{1,0:T(8,128)(2,1)S(1)} %add.5), channel_id=1, source_target_pairs={{0,2},{2,3},{3,1},{1,0},{4,6},{6,7},{7,5},{5,4},{8,10},{10,11},{11... | collective-permute-start | bytes 786440 | tf_op jit(solution)/shard_map/ppermute | solution.py:538
  71.3 24.5 %collective-permute-start.3 = (bf16[128,2048]{1,0:T(8,128)(2,1)S(1)}, bf16[128,2048]{1,0:T(8,128)(2,1)S(1)}, u32[]{:S(2)}, u32[]{:S(2)}) collective-permute-start(bf16[128,2048]{1,0:T(8,128)(2,1)S(1)} %project.5), channel_id=1, source_target_pairs={{0,24},{4,28},{8,16},{12,20},{16,8},{20,12},{24,0},{28,4},{1,25},{... | collective-permute-start | bytes 1572872 | tf_op jit(solution)/shard_map/ppermute | solution.py:505
  73.8 23.2 %collective-permute-start.14 = (bf16[128,2048]{1,0:T(8,128)(2,1)S(1)}, bf16[128,2048]{1,0:T(8,128)(2,1)S(1)}, u32[]{:S(2)}, u32[]{:S(2)}) collective-permute-start(bf16[128,2048]{1,0:T(8,128)(2,1)S(1)} %project.6), channel_id=1, source_target_pairs={{0,28},{4,24},{8,20},{12,16},{16,12},{20,8},{24,4},{28,0},{1,29},{... | collective-permute-start | bytes 1572872 | tf_op jit(solution)/shard_map/ppermute | solution.py:505
  75.8 10.2 %collective-permute-start.20 = (bf16[64,2048]{1,0:T(8,128)(2,1)S(1)}, bf16[64,2048]{1,0:T(8,128)(2,1)S(1)}, u32[]{:S(2)}, u32[]{:S(2)}) collective-permute-start(bf16[64,2048]{1,0:T(8,128)(2,1)S(1)} %add.4), channel_id=1, source_target_pairs={{0,2},{2,3},{3,1},{1,0},{4,6},{6,7},{7,5},{5,4},{8,10},{10,11},{11... | collective-permute-start | bytes 786440 | tf_op jit(solution)/shard_map/ppermute | solution.py:538
  83.1 16.0 %collective-permute-start.16 = (bf16[128,2048]{1,0:T(8,128)(2,1)S(1)}, bf16[128,2048]{1,0:T(8,128)(2,1)S(1)}, u32[]{:S(2)}, u32[]{:S(2)}) collective-permute-start(bf16[128,2048]{1,0:T(8,128)(2,1)S(1)} %project.7), channel_id=1, source_target_pairs={{0,16},{4,20},{8,24},{12,28},{16,0},{20,4},{24,8},{28,12},{1,17},{... | collective-permute-start | bytes 1572872 | tf_op jit(solution)/shard_map/ppermute | solution.py:505
  86.0 11.0 %collective-permute-start.19 = (bf16[64,2048]{1,0:T(8,128)(2,1)S(1)}, bf16[64,2048]{1,0:T(8,128)(2,1)S(1)}, u32[]{:S(2)}, u32[]{:S(2)}) collective-permute-start(bf16[64,2048]{1,0:T(8,128)(2,1)S(1)} %add.6), channel_id=1, source_target_pairs={{0,18},{2,19},{3,17},{1,16},{16,2},{18,3},{19,1},{17,0},{4,22},{6,... | collective-permute-start | bytes 786440 | tf_op jit(solution)/shard_map/ppermute | solution.py:537
  87.4 11.7 %collective-permute-start.21 = (bf16[64,2048]{1,0:T(8,128)(2,1)S(1)}, bf16[64,2048]{1,0:T(8,128)(2,1)S(1)}, u32[]{:S(2)}, u32[]{:S(2)}) collective-permute-start(bf16[64,2048]{1,0:T(8,128)(2,1)S(1)} %add.7), channel_id=1, source_target_pairs={{0,18},{2,19},{3,17},{1,16},{16,2},{18,3},{19,1},{17,0},{4,22},{6,... | collective-permute-start | bytes 786440 | tf_op jit(solution)/shard_map/ppermute | solution.py:537
